TPU v7x, 32 devices: a whole 2x2x4 slice. The times are simulated.
32 devices in a mesh: shard: 4 (over y, x), ctx: 2 (over core), tp: 4 (over z).
Axes of the slice: x: 2, y: 2, z: 4, core: 2. Of those that a mesh axis runs over, the one named last changes fastest.
Arguments:
- tokens: bfloat16 [8192, 1024], P(('shard', 'ctx')), may hold values from -6 to 6
- segment_ids: int32 [4, 2048], P('shard'), may hold values from 0 to 3, never falling along the last dimension, each value on 1 to 1024 neighbouring positions
- cotangent: bfloat16 [8192, 1024], P(('shard', 'ctx')), may hold values from -6 to 6
- mixer_gain: float32 [1024], replicated, may hold values from 0.5 to 1.5
- query_weight: bfloat16 [1024, 1024], P('shard', 'tp'), may hold values from -0.1875 to 0.1875
- key_weight: bfloat16 [1024, 1024], P('shard', 'tp'), may hold values from -0.1875 to 0.1875
- value_weight: bfloat16 [1024, 2048], P('shard', 'tp'), may hold values from -0.1875 to 0.1875
- gate_weight: bfloat16 [1024, 2048], P('shard', 'tp'), may hold values from -0.1875 to 0.1875
- decay_weight: bfloat16 [1024, 8], P('shard', 'tp'), may hold values from -0.1875 to 0.1875
- beta_weight: bfloat16 [1024, 8], P('shard', 'tp'), may hold values from -0.1875 to 0.1875
- query_conv: float32 [4, 1024], P(None, 'tp'), may hold values from -2 to 2
- key_conv: float32 [4, 1024], P(None, 'tp'), may hold values from -2 to 2
- value_conv: float32 [4, 2048], P(None, 'tp'), may hold values from -2 to 2
- decay_log: float32 [8], P('tp'), may hold values from -7.6 to -2.3
- decay_bias: float32 [8], P('tp'), may hold values from -3 to 3
- out_gain: float32 [256], replicated, may hold values from 0.5 to 1.5
- output_weight: bfloat16 [2048, 1024], P('tp', 'shard'), may hold values from -0.1875 to 0.1875
- hidden_gain: float32 [1024], replicated, may hold values from 0.5 to 1.5
- hidden_gate: bfloat16 [1024, 2816], P('shard', 'tp'), may hold values from -0.1875 to 0.1875
- hidden_up: bfloat16 [1024, 2816], P('shard', 'tp'), may hold values from -0.1875 to 0.1875
- hidden_down: bfloat16 [2816, 1024], P('tp', 'shard'), may hold values from -0.15625 to 0.15625
Outputs:
- block_out: bfloat16 [8192, 1024], P(('shard', 'ctx'))
- input_grad: float32 [8192, 1024], P(('shard', 'ctx'))
- mixer_gain_grad: float32 [1024], replicated
- query_weight_grad: float32 [1024, 1024], P('shard', 'tp')
- key_weight_grad: float32 [1024, 1024], P('shard', 'tp')
- value_weight_grad: float32 [1024, 2048], P('shard', 'tp')
- gate_weight_grad: float32 [1024, 2048], P('shard', 'tp')
- decay_weight_grad: float32 [1024, 8], P('shard', 'tp')
- beta_weight_grad: float32 [1024, 8], P('shard', 'tp')
- query_conv_grad: float32 [4, 1024], P(None, 'tp')
- key_conv_grad: float32 [4, 1024], P(None, 'tp')
- value_conv_grad: float32 [4, 2048], P(None, 'tp')
- decay_log_grad: float32 [8], P('tp')
- decay_bias_grad: float32 [8], P('tp')
- out_gain_grad: float32 [256], replicated
- output_weight_grad: float32 [2048, 1024], P('tp', 'shard')
- hidden_gain_grad: float32 [1024], replicated
- hidden_gate_grad: float32 [1024, 2816], P('shard', 'tp')
- hidden_up_grad: float32 [1024, 2816], P('shard', 'tp')
- hidden_down_grad: float32 [2816, 1024], P('tp', 'shard')
Inputs may be any that keep to these rules, and one draw needn't show every extreme that they name: `segment_ids`: within each packed row the document numbers never fall; each document has 1 to 1024 tokens and one has exactly 1024.
All inputs are finite; a program needn't handle non-finite values.
Results may differ from a plain program's by a relative error of at most 0.015.
The roundings to bfloat16 on the way count: a program that leaves them out, or rounds other values in their place, can miss the bound.
Values may be sent and summed in bfloat16 or wider, within the bound.
A program may use at most 256 MiB of HBM per device.

v0:
```python
import jax
import jax.numpy as jnp
from jax import lax
from jax.sharding import PartitionSpec as P

GROUP = 64


HIGH = lax.Precision.HIGHEST


def from_behind(block, axis, distance):
    devices = range(lax.axis_size(axis))
    route = [(i - distance, i) for i in devices if i - distance in devices]
    return lax.ppermute(block, axis, route)


def dot_plain(left, right):
    return jnp.dot(left, right, preferred_element_type=jnp.float32)


def dot_first(left, right):
    return lax.dot_general(
        left, right, (((0,), (0,)), ((), ())), preferred_element_type=jnp.float32
    )


def dot_second(left, right):
    return lax.dot_general(
        left, right, (((1,), (1,)), ((), ())), preferred_element_type=jnp.float32
    )


def rms_norm(values, gain):
    return values * lax.rsqrt(jnp.mean(values * values, axis=-1, keepdims=True) + 1e-06) * gain


def unit_rows(values):
    return values * lax.rsqrt(jnp.sum(values * values, axis=-1, keepdims=True) + 1e-06)


def convolve(projected, rim_rows, weights, seg_ext):
    tok_rows = projected.shape[0]
    taps = weights.shape[0]
    extended = jnp.concatenate([rim_rows, projected], axis=0)
    seg_now = seg_ext[taps - 1 :]
    summed = jnp.zeros_like(projected)
    for offset in range(taps):
        begin = taps - 1 - offset
        linked = (seg_ext[begin : begin + tok_rows] == seg_now).astype(jnp.float32)
        summed = summed + weights[offset] * extended[begin : begin + tok_rows] * linked[:, None]
    return jax.nn.silu(summed)


def group_step(state, inputs):
    query, keys, values, beta, log_gate, seg_now, seg_before = inputs
    block_len = query.shape[0]
    cumul = jnp.cumsum(log_gate, axis=0).T
    order = jnp.arange(block_len)
    causal = (order[:, None] >= order[None, :]) & (seg_now[:, None] == seg_now[None, :])
    strict = causal & (order[:, None] > order[None, :])
    spacing = cumul[:, :, None] - cumul[:, None, :]
    within = jnp.where(causal, jnp.exp(jnp.where(causal, spacing, 0.0)), 0.0)
    from_start = jnp.where((seg_now == seg_before)[None, :], jnp.exp(cumul), 0.0)
    to_end = within[:, -1, :]
    query_heads = jnp.transpose(query, (1, 0, 2))
    key_heads = jnp.transpose(keys, (1, 0, 2))
    value_heads = jnp.transpose(values, (1, 0, 2))
    beta_heads = beta.T
    key_dots = jnp.einsum("htd,hsd->hts", key_heads, key_heads, precision=HIGH)
    system = jnp.eye(block_len, dtype=jnp.float32)[None] + jnp.where(
        strict, beta_heads[:, :, None] * within * key_dots, 0.0
    )
    fresh = jax.scipy.linalg.solve_triangular(
        system, beta_heads[:, :, None] * value_heads, lower=True, unit_diagonal=True
    )
    spread = jax.scipy.linalg.solve_triangular(
        system, (beta_heads * from_start)[:, :, None] * key_heads, lower=True, unit_diagonal=True
    )
    update = fresh - jnp.einsum("hcd,hrd->hcr", spread, state, precision=HIGH)
    scores = jnp.einsum("htd,hsd->hts", query_heads, key_heads, precision=HIGH) * within
    outputs = from_start[:, :, None] * jnp.einsum(
        "hcd,hrd->hcr", query_heads, state, precision=HIGH
    )
    outputs = outputs + jnp.einsum("hts,hsr->htr", scores, update, precision=HIGH)
    new_state = from_start[:, -1][:, None, None] * state
    new_state = new_state + jnp.einsum(
        "hcr,hcd->hrd", update * to_end[:, :, None], key_heads, precision=HIGH
    )
    return (new_state, jnp.transpose(outputs, (1, 0, 2)))


def prepare(floats, seg_ext, key_dim, block_len):
    (
        q_proj,
        k_proj,
        v_proj,
        q_rim,
        k_rim,
        v_rim,
        a_proj,
        b_proj,
        q_conv,
        k_conv,
        v_conv,
        decay_log,
        decay_bias,
    ) = floats
    tok_rows = q_proj.shape[0]
    num_heads = a_proj.shape[1]
    taps = q_conv.shape[0]
    query = unit_rows(
        convolve(q_proj, q_rim, q_conv, seg_ext).reshape(tok_rows, num_heads, key_dim)
    ) * key_dim ** (-0.5)
    keys = unit_rows(convolve(k_proj, k_rim, k_conv, seg_ext).reshape(tok_rows, num_heads, key_dim))
    values = convolve(v_proj, v_rim, v_conv, seg_ext).reshape(tok_rows, num_heads, -1)
    val_dim = values.shape[2]
    beta = jax.nn.sigmoid(b_proj)
    log_gate = -jnp.exp(decay_log) * jax.nn.softplus(a_proj + decay_bias)
    widened = jnp.concatenate(
        [jnp.zeros((tok_rows, num_heads, key_dim), jnp.float32), values], axis=-1
    )
    blocks = tok_rows // block_len
    seg_now = seg_ext[taps - 1 :].reshape(blocks, block_len)
    seg_before = seg_ext[taps - 2 : taps - 2 + tok_rows : block_len]
    start_state = jnp.concatenate(
        [
            jnp.broadcast_to(jnp.eye(key_dim, dtype=jnp.float32), (num_heads, key_dim, key_dim)),
            jnp.zeros((num_heads, val_dim, key_dim), jnp.float32),
        ],
        axis=1,
    )

    def split(array):
        return array.reshape((blocks, block_len) + array.shape[1:])

    final_state, outputs = lax.scan(
        group_step,
        start_state,
        (
            split(query),
            split(keys),
            split(widened),
            split(beta),
            split(log_gate),
            seg_now,
            seg_before,
        ),
    )
    outputs = outputs.reshape(tok_rows, num_heads, key_dim + val_dim)
    return (
        outputs[..., :key_dim],
        outputs[..., key_dim:],
        final_state[:, :key_dim],
        final_state[:, key_dim:],
    )


def gated_out(core, gate_proj, gain):
    tok_rows = core.shape[0]
    gating = jax.nn.silu(gate_proj.reshape(core.shape))
    return (rms_norm(core, gain) * gating).reshape(tok_rows, -1)


def swish_product(gate_pre, up_pre):
    return jax.nn.silu(gate_pre) * up_pre


def add_tail(grad_rows, incoming):
    width = incoming.shape[0]
    return jnp.concatenate([grad_rows[:-width], grad_rows[-width:] + incoming], axis=0)


def body(
    tokens,
    segment_ids,
    cotangent,
    mixer_gain,
    query_weight,
    key_weight,
    value_weight,
    gate_weight,
    decay_weight,
    beta_weight,
    query_conv,
    key_conv,
    value_conv,
    decay_log,
    decay_bias,
    out_gain,
    output_weight,
    hidden_gain,
    hidden_gate,
    hidden_up,
    hidden_down,
):
    tok_rows = tokens.shape[0]
    num_heads = decay_log.shape[0]
    key_dim = query_weight.shape[1] // num_heads
    taps = query_conv.shape[0]
    range_count = lax.axis_size("ctx")
    begin_row = lax.axis_index("ctx") * tok_rows
    seg_pad = jnp.concatenate([jnp.full((taps - 1,), -1, jnp.int32), segment_ids[0]])
    seg_ext = lax.dynamic_slice_in_dim(seg_pad, begin_row, tok_rows + taps - 1)
    (
        query_full,
        key_full,
        value_full,
        gate_full,
        decay_full,
        beta_full,
        output_full,
        inner_gate,
        inner_up,
        inner_down,
    ) = (
        lax.all_gather(query_weight, "shard", axis=0, tiled=True),
        lax.all_gather(key_weight, "shard", axis=0, tiled=True),
        lax.all_gather(value_weight, "shard", axis=0, tiled=True),
        lax.all_gather(gate_weight, "shard", axis=0, tiled=True),
        lax.all_gather(decay_weight, "shard", axis=0, tiled=True),
        lax.all_gather(beta_weight, "shard", axis=0, tiled=True),
        lax.all_gather(output_weight, "shard", axis=1, tiled=True),
        lax.all_gather(hidden_gate, "shard", axis=0, tiled=True),
        lax.all_gather(hidden_up, "shard", axis=0, tiled=True),
        lax.all_gather(hidden_down, "shard", axis=1, tiled=True),
    )
    x_float = tokens.astype(jnp.float32)
    normed, norm_pull = jax.vjp(rms_norm, x_float, mixer_gain)
    normed_low = normed.astype(jnp.bfloat16)
    q_proj = dot_plain(normed_low, query_full)
    k_proj = dot_plain(normed_low, key_full)
    v_proj = dot_plain(normed_low, value_full)
    z_proj = dot_plain(normed_low, gate_full)
    a_proj = dot_plain(normed_low, decay_full)
    b_proj = dot_plain(normed_low, beta_full)
    q_rim, k_rim, v_rim = from_behind(
        (
            q_proj[tok_rows - taps + 1 :],
            k_proj[tok_rows - taps + 1 :],
            v_proj[tok_rows - taps + 1 :],
        ),
        "ctx",
        1,
    )

    def local_mixer(floats):
        return prepare(floats, seg_ext, key_dim, GROUP)

    (mapped_query, base_query, state_map, state_base), prep_pull = jax.vjp(
        local_mixer,
        (
            q_proj,
            k_proj,
            v_proj,
            q_rim,
            k_rim,
            v_rim,
            a_proj,
            b_proj,
            query_conv,
            key_conv,
            value_conv,
            decay_log,
            decay_bias,
        ),
    )

    def forward_link(index, carried):
        ends = jnp.einsum("hvd,hde->hve", carried, state_map, precision=HIGH) + state_base
        return from_behind(ends, "ctx", 1)

    state_in = lax.fori_loop(0, range_count - 1, forward_link, jnp.zeros_like(state_base))
    core = base_query + jnp.einsum("hvd,rhd->rhv", state_in, mapped_query, precision=HIGH)
    mixed, post_pull = jax.vjp(gated_out, core, z_proj, out_gain)
    mixed_low = mixed.astype(jnp.bfloat16)
    attn = lax.psum(dot_plain(mixed_low, output_full), "tp")
    middle = x_float + attn
    normed2, norm2_pull = jax.vjp(rms_norm, middle, hidden_gain)
    normed2_low = normed2.astype(jnp.bfloat16)
    gate_pre = dot_plain(normed2_low, inner_gate)
    up_pre = dot_plain(normed2_low, inner_up)
    act, act_pull = jax.vjp(swish_product, gate_pre, up_pre)
    act_low = act.astype(jnp.bfloat16)
    ffn = lax.psum(dot_plain(act_low, inner_down).astype(jnp.bfloat16), "tp").astype(jnp.float32)
    block_out = (middle + ffn).astype(jnp.bfloat16)
    cot_float = cotangent.astype(jnp.float32)
    grad_down = dot_first(act_low, cotangent)
    grad_act = dot_second(cotangent, inner_down)
    grad_gate, grad_up = act_pull(grad_act)
    gate_low = grad_gate.astype(jnp.bfloat16)
    up_low = grad_up.astype(jnp.bfloat16)
    grad_inner_gate = dot_first(normed2_low, gate_low)
    grad_inner_up = dot_first(normed2_low, up_low)
    part_second = dot_second(gate_low, inner_gate) + dot_second(up_low, inner_up)
    grad_normed2 = lax.psum(part_second, "tp")
    grad_mid_norm, grad_hidden_gain = norm2_pull(grad_normed2)
    grad_middle = cot_float + grad_mid_norm
    attn_low = grad_middle.astype(jnp.bfloat16)
    grad_output = dot_first(mixed_low, attn_low)
    grad_mixed = dot_second(attn_low, output_full)
    grad_core, grad_z, grad_out_gain = post_pull(grad_mixed)
    direct = jnp.einsum("rhv,rhd->hvd", grad_core, mapped_query, precision=HIGH)

    def backward_link(index, carried):
        totals = jnp.einsum("hve,hde->hvd", carried, state_map, precision=HIGH) + direct
        return from_behind(totals.astype(jnp.bfloat16), "ctx", -1).astype(totals.dtype)

    grad_end = lax.fori_loop(0, range_count - 1, backward_link, jnp.zeros_like(direct))
    grad_mapped = jnp.einsum("rhv,hvd->rhd", grad_core, state_in, precision=HIGH)
    grad_map = jnp.einsum("hvd,hve->hde", state_in, grad_end, precision=HIGH)
    (float_grads,) = prep_pull((grad_mapped, grad_core, grad_map, grad_end))
    (
        grad_q,
        grad_k,
        grad_v,
        grad_q_rim,
        grad_k_rim,
        grad_v_rim,
        grad_a,
        grad_b,
        grad_q_conv,
        grad_k_conv,
        grad_v_conv,
        grad_decay_log,
        grad_decay_bias,
    ) = float_grads
    back_q, back_k, back_v = from_behind((grad_q_rim, grad_k_rim, grad_v_rim), "ctx", -1)
    q_low = add_tail(grad_q, back_q).astype(jnp.bfloat16)
    k_low = add_tail(grad_k, back_k).astype(jnp.bfloat16)
    v_low = add_tail(grad_v, back_v).astype(jnp.bfloat16)
    z_low = grad_z.astype(jnp.bfloat16)
    a_low = grad_a.astype(jnp.bfloat16)
    b_low = grad_b.astype(jnp.bfloat16)
    grad_query = dot_first(normed_low, q_low)
    grad_key = dot_first(normed_low, k_low)
    grad_value = dot_first(normed_low, v_low)
    grad_gate_proj = dot_first(normed_low, z_low)
    grad_decay = dot_first(normed_low, a_low)
    grad_beta = dot_first(normed_low, b_low)
    part_first = (
        dot_second(q_low, query_full) + dot_second(k_low, key_full) + dot_second(v_low, value_full)
    )
    part_first = (
        part_first
        + dot_second(z_low, gate_full)
        + dot_second(a_low, decay_full)
        + dot_second(b_low, beta_full)
    )
    grad_normed, out_gain_total = (
        lax.psum(part_first.astype(jnp.bfloat16), "tp").astype(jnp.float32),
        lax.psum(grad_out_gain.astype(jnp.bfloat16), "tp").astype(jnp.float32),
    )
    grad_x_norm, grad_mixer_gain = norm_pull(grad_normed)
    input_grad = grad_middle + grad_x_norm
    scattered = (
        lax.psum_scatter(
            grad_query.astype(jnp.bfloat16), "shard", scatter_dimension=0, tiled=True
        ).astype(jnp.float32),
        lax.psum_scatter(
            grad_key.astype(jnp.bfloat16), "shard", scatter_dimension=0, tiled=True
        ).astype(jnp.float32),
        lax.psum_scatter(
            grad_value.astype(jnp.bfloat16), "shard", scatter_dimension=0, tiled=True
        ).astype(jnp.float32),
        lax.psum_scatter(
            grad_gate_proj.astype(jnp.bfloat16), "shard", scatter_dimension=0, tiled=True
        ).astype(jnp.float32),
        lax.psum_scatter(
            grad_decay.astype(jnp.bfloat16), "shard", scatter_dimension=0, tiled=True
        ).astype(jnp.float32),
        lax.psum_scatter(
            grad_beta.astype(jnp.bfloat16), "shard", scatter_dimension=0, tiled=True
        ).astype(jnp.float32),
        lax.psum_scatter(
            grad_output.astype(jnp.bfloat16), "shard", scatter_dimension=1, tiled=True
        ).astype(jnp.float32),
        lax.psum_scatter(
            grad_inner_gate.astype(jnp.bfloat16), "shard", scatter_dimension=0, tiled=True
        ).astype(jnp.float32),
        lax.psum_scatter(
            grad_inner_up.astype(jnp.bfloat16), "shard", scatter_dimension=0, tiled=True
        ).astype(jnp.float32),
        lax.psum_scatter(
            grad_down.astype(jnp.bfloat16), "shard", scatter_dimension=1, tiled=True
        ).astype(jnp.float32),
    )
    (
        sum_query,
        sum_key,
        sum_value,
        sum_gate,
        sum_decay,
        sum_beta,
        sum_output,
        sum_inner_gate,
        sum_inner_up,
        sum_down,
    ) = (
        lax.psum(scattered[0].astype(jnp.bfloat16), "ctx").astype(jnp.float32),
        lax.psum(scattered[1].astype(jnp.bfloat16), "ctx").astype(jnp.float32),
        lax.psum(scattered[2].astype(jnp.bfloat16), "ctx").astype(jnp.float32),
        lax.psum(scattered[3].astype(jnp.bfloat16), "ctx").astype(jnp.float32),
        lax.psum(scattered[4].astype(jnp.bfloat16), "ctx").astype(jnp.float32),
        lax.psum(scattered[5].astype(jnp.bfloat16), "ctx").astype(jnp.float32),
        lax.psum(scattered[6].astype(jnp.bfloat16), "ctx").astype(jnp.float32),
        lax.psum(scattered[7].astype(jnp.bfloat16), "ctx").astype(jnp.float32),
        lax.psum(scattered[8].astype(jnp.bfloat16), "ctx").astype(jnp.float32),
        lax.psum(scattered[9].astype(jnp.bfloat16), "ctx").astype(jnp.float32),
    )
    (
        sum_mixer_gain,
        sum_hidden_gain,
        sum_out_gain,
        sum_q_conv,
        sum_k_conv,
        sum_v_conv,
        sum_decay_log,
        sum_decay_bias,
    ) = lax.psum(
        (
            grad_mixer_gain,
            grad_hidden_gain,
            out_gain_total,
            grad_q_conv,
            grad_k_conv,
            grad_v_conv,
            grad_decay_log,
            grad_decay_bias,
        ),
        ("shard", "ctx"),
    )
    return (
        block_out,
        input_grad,
        sum_mixer_gain,
        sum_query,
        sum_key,
        sum_value,
        sum_gate,
        sum_decay,
        sum_beta,
        sum_q_conv,
        sum_k_conv,
        sum_v_conv,
        sum_decay_log,
        sum_decay_bias,
        sum_out_gain,
        sum_output,
        sum_hidden_gain,
        sum_inner_gate,
        sum_inner_up,
        sum_down,
    )


def solution(mesh):
    in_specs = (
        P(("shard", "ctx"), None),
        P("shard", None),
        P(("shard", "ctx"), None),
        P(),
        P("shard", "tp"),
        P("shard", "tp"),
        P("shard", "tp"),
        P("shard", "tp"),
        P("shard", "tp"),
        P("shard", "tp"),
        P(None, "tp"),
        P(None, "tp"),
        P(None, "tp"),
        P("tp"),
        P("tp"),
        P(),
        P("tp", "shard"),
        P(),
        P("shard", "tp"),
        P("shard", "tp"),
        P("tp", "shard"),
    )
    out_specs = (
        P(("shard", "ctx"), None),
        P(("shard", "ctx"), None),
        P(),
        P("shard", "tp"),
        P("shard", "tp"),
        P("shard", "tp"),
        P("shard", "tp"),
        P("shard", "tp"),
        P("shard", "tp"),
        P(None, "tp"),
        P(None, "tp"),
        P(None, "tp"),
        P("tp"),
        P("tp"),
        P(),
        P("tp", "shard"),
        P(),
        P("shard", "tp"),
        P("shard", "tp"),
        P("tp", "shard"),
    )
    return jax.shard_map(body, mesh=mesh, in_specs=in_specs, out_specs=out_specs, check_vma=False)
```

profile of v0, /device:TPU:0, one launch (start us, length us, event | category | flops | bytes accessed | tf_op | source)
XLA Modules:
  0.0 2531.8 jit_solution(6565583478325132112)
XLA Ops:
  8.7 12.0 all_gather.32
  27.4 12.9 all_gather.34
  113.9 575.2 %while.110 = (s32[]{:T(128)}, f32[2,384,128]{2,1,0:T(8,128)S(1)}, f32[16,64,2,384]{3,1,0,2:T(8,128)}, pred[16,2,64,64]{3,2,1,0:T(32,128)(4,1)}, f32[16,2,64,64]{...) while((s32[]{:T(128)}, f32[2,384,128]{2,1,0:T(8,128)S(1)}, ...), condition=%wide.region_5.6_spmd.clone, body=%wide.region_3.5_spmd.clone.sunk | while | flops 340500864 | bytes 7225429 | solution.py:137
  714.8 153.0 %all-reduce.42.cloned.1.call-done = f32[1024,1024]{1,0:T(8,128)} async-done(((f32[1024,1024]{1,0:T(8,128)}), f32[1024,1024]{1,0:T(8,128)}) %all-reduce.42.cloned.1.call-update) | async-done | bytes 4194320 | tf_op jit(solution)/shard_map/psum | solution.py:277
  875.1 23.3 all-gather.13.cloned.1.call-done
  903.7 26.3 %all-gather.15.cloned.1.call-done = bf16[1024,704]{0,1:T(8,128)(2,1)} async-done(((bf16[256,704]{0,1:T(8,128)(2,1)}), bf16[1024,704]{0,1:T(8,128)(2,1)}) %all-gather.15.cloned.1.call-update) | async-done | bytes 1441808 | tf_op jit(solution)/shard_map/all_gather | solution.py:225
  935.3 26.4 %all-gather.17.cloned.1.call-done = bf16[704,1024]{1,0:T(8,128)(2,1)} async-done(((bf16[704,256]{1,0:T(8,128)(2,1)}), bf16[704,1024]{1,0:T(8,128)(2,1)}) %all-gather.17.cloned.1.call-update) | async-done | bytes 1441808 | tf_op jit(solution)/shard_map/all_gather | solution.py:226
  992.3 138.6 %all-reduce.44.cloned.1.call-done = f32[1024,1024]{1,0:T(8,128)} async-done(((f32[1024,1024]{1,0:T(8,128)}), f32[1024,1024]{1,0:T(8,128)}) %all-reduce.44.cloned.1.call-update) | async-done | bytes 4194320 | tf_op jit(solution)/shard_map/psum | solution.py:296
  1167.3 924.6 %while.111 = (s32[]{:T(128)}, f32[2,384,128]{2,1,0:T(8,128)S(1)}, f32[16,64,2,128]{3,1,2,0:T(8,128)}, f32[16,64,2,128]{3,1,2,0:T(8,128)}, f32[16,64,2,384]{3,1,0...) while((s32[]{:T(128)}, f32[2,384,128]{2,1,0:T(8,128)S(1)}, ...), condition=%wide.region_23.25_spmd.clone.clone, body=%wide.region_13.24_spmd.clone.clone.sunk | while | flops 693555648 | bytes 11178601 | solution.py:137
  1190.8 10.6 custom-call.68
  1248.6 10.6 custom-call.68
  1421.9 10.6 custom-call.68
  1768.4 10.6 custom-call.68
  1826.1 10.6 custom-call.68
  1941.6 10.6 custom-call.68
  2057.2 10.6 custom-call.68
  2178.1 27.1 %reduce-scatter.23.cloned.1.call-done = bf16[512,256]{1,0:T(8,128)(2,1)} async-done(((bf16[512,1024]{1,0:T(8,128)(2,1)}), bf16[512,256]{1,0:T(8,128)(2,1)}) %reduce-scatter.23.cloned.1.call-update) | async-done | bytes 262160 | tf_op jit(solution)/shard_map/reduce_scatter | solution.py:375
  2205.1 30.5 %reduce-scatter.21.cloned.1.call-done = bf16[256,512]{1,0:T(8,128)(2,1)} async-done(((bf16[1024,512]{1,0:T(8,128)(2,1)}), bf16[256,512]{1,0:T(8,128)(2,1)}) %reduce-scatter.21.cloned.1.call-update) | async-done | bytes 262160 | tf_op jit(solution)/shard_map/reduce_scatter | solution.py:366
  2235.6 30.8 %reduce-scatter.19.cloned.1.call-done = bf16[256,512]{1,0:T(8,128)(2,1)} async-done(((bf16[1024,512]{1,0:T(8,128)(2,1)}), bf16[256,512]{1,0:T(8,128)(2,1)}) %reduce-scatter.19.cloned.1.call-update) | async-done | bytes 262160 | tf_op jit(solution)/shard_map/reduce_scatter | solution.py:363
  2266.4 11.7 psum.177
  2278.2 15.5 reduce-scatter.31.cloned.1.call-done
  2294.6 26.6 %reduce-scatter.33.cloned.1.call-done = bf16[256,2]{1,0:T(8,128)(2,1)} async-done(((bf16[1024,2]{1,0:T(8,128)(2,1)}), bf16[256,2]{1,0:T(8,128)(2,1)}) %reduce-scatter.33.cloned.1.call-update) | async-done | bytes 1040
  2325.8 153.8 %all-reduce.46.cloned.1.call-done = (bf16[1024,1024]{1,0:T(8,128)(2,1)}, bf16[1024,1024]{1,0:T(8,128)(2,1)}) async-done(((bf16[1024,1024]{1,0:T(8,128)(2,1)}, bf16[1024,1024]{1,0:T(8,128)(2,1)}), (bf16[1024,1024]{1,0:T(8,128)(2,1)}, bf16[1024,1024]{1,0:T(8,128)(2,1)})) %all-reduce.46.cloned.1.call-update) | async-done | bytes 4194320 | tf_op jit(solution)/shard_map/psum | solution.py:285
  2482.9 25.1 all-reduce.33
  (1725 shorter events, 1724.2 us)
Async XLA Ops:
  7.2 94.2 %all-gather.7.cloned.1.call-start = ((), (), s32[]{:S(2)}) async-start(), calls=%async_computation.10 | async-start | bytes 1310720 | tf_op jit(solution)/shard_map/all_gather | solution.py:219
  7.9 684.2 %all-gather.9.cloned.1.call-start = ((), (), s32[]{:S(2)}) async-start(), calls=%async_computation.11 | async-start | bytes 1310720 | tf_op jit(solution)/shard_map/all_gather | solution.py:220
  8.7 698.8 %all-gather.11.cloned.1.call-start = ((), (), s32[]{:S(2)}) async-start(), calls=%async_computation.12 | async-start | bytes 1310720 | tf_op jit(solution)/shard_map/all_gather | solution.py:223
  25.6 41.4 %collective-permute-start = (f32[3,256]{1,0:T(4,128)}, f32[3,256]{1,0:T(4,128)}, u32[]{:S(2)}, u32[]{:S(2)}) collective-permute-start(f32[3,256]{1,0:T(4,128)} %slice.231), channel_id=1, source_target_pairs={{0,4},{1,5},{2,6},{3,7},{8,12},{9,13},{10,14},{11,15},{16,20},{17,... | collective-permute-start | bytes 9224 | tf_op jit(solution)/shard_map/ppermute | solution.py:15
  42.7 31.1 %collective-permute-start.2 = (f32[3,256]{1,0:T(4,128)}, f32[3,256]{1,0:T(4,128)}, u32[]{:S(2)}, u32[]{:S(2)}) collective-permute-start(f32[3,256]{1,0:T(4,128)} %slice.241), channel_id=1, source_target_pairs={{0,4},{1,5},{2,6},{3,7},{8,12},{9,13},{10,14},{11,15},{16,20},{17,... | collective-permute-start | bytes 9224 | tf_op jit(solution)/shard_map/ppermute | solution.py:15
  44.6 823.1 %all-reduce.42.cloned.1.call-start = ((), (), s32[]{:S(2)}) async-start(), calls=%async_computation.13 | async-start | bytes 8388608 | tf_op jit(solution)/shard_map/psum | solution.py:277
  690.7 8.2 collective-permute-start.3
  712.4 186.0 %all-gather.13.cloned.1.call-start = ((), (), s32[]{:S(2)}) async-start(), calls=%async_computation.14 | async-start | bytes 1802240 | tf_op jit(solution)/shard_map/all_gather | solution.py:224
  713.0 217.1 %all-gather.15.cloned.1.call-start = ((), (), s32[]{:S(2)}) async-start(), calls=%async_computation.15 | async-start | bytes 1802240 | tf_op jit(solution)/shard_map/all_gather | solution.py:225
  713.5 248.2 %all-gather.17.cloned.1.call-start = ((), (), s32[]{:S(2)}) async-start(), calls=%async_computation.16 | async-start | bytes 1802240 | tf_op jit(solution)/shard_map/all_gather | solution.py:226
  714.3 416.6 %all-reduce.44.cloned.1.call-start = ((), (), s32[]{:S(2)}) async-start(), calls=%async_computation.17 | async-start | bytes 8388608 | tf_op jit(solution)/shard_map/psum | solution.py:296
  975.8 1202.2 %reduce-scatter.27.cloned.1.call-start = ((), (), s32[]{:S(2)}) async-start(), calls=%async_computation.24 | async-start | bytes 1802240 | tf_op jit(solution)/shard_map/reduce_scatter | solution.py:381
  980.7 1197.3 %reduce-scatter.25.cloned.1.call-start = ((), (), s32[]{:S(2)}) async-start(), calls=%async_computation.23 | async-start | bytes 1802240 | tf_op jit(solution)/shard_map/reduce_scatter | solution.py:378
  986.2 1191.8 %reduce-scatter.29.cloned.1.call-start = ((), (), s32[]{:S(2)}) async-start(), calls=%async_computation.25 | async-start | bytes 1802240 | tf_op jit(solution)/shard_map/reduce_scatter | solution.py:384
  992.3 1185.8 %reduce-scatter.17.cloned.1.call-start = ((), (), s32[]{:S(2)}) async-start(), calls=%async_computation.19 | async-start | bytes 655360 | tf_op jit(solution)/shard_map/reduce_scatter | solution.py:360
  1156.7 5.2 collective-permute-start.4
  2121.9 56.2 %reduce-scatter.15.cloned.1.call-start = ((), (), s32[]{:S(2)}) async-start(), calls=%async_computation.18 | async-start | bytes 655360 | tf_op jit(solution)/shard_map/reduce_scatter | solution.py:357
  2127.6 77.5 %reduce-scatter.23.cloned.1.call-start = ((), (), s32[]{:S(2)}) async-start(), calls=%async_computation.22 | async-start | bytes 1310720 | tf_op jit(solution)/shard_map/reduce_scatter | solution.py:375
  2132.2 103.5 %reduce-scatter.21.cloned.1.call-start = ((), (), s32[]{:S(2)}) async-start(), calls=%async_computation.21 | async-start | bytes 1310720 | tf_op jit(solution)/shard_map/reduce_scatter | solution.py:366
  2136.1 130.3 %reduce-scatter.19.cloned.1.call-start = ((), (), s32[]{:S(2)}) async-start(), calls=%async_computation.20 | async-start | bytes 1310720 | tf_op jit(solution)/shard_map/reduce_scatter | solution.py:363
  2148.9 144.8 %reduce-scatter.31.cloned.1.call-start = ((), (), s32[]{:S(2)}) async-start(), calls=%async_computation.26 | async-start | bytes 327680
  2166.0 155.3 %reduce-scatter.33.cloned.1.call-start = ((), (), s32[]{:S(2)}) async-start(), calls=%async_computation.27 | async-start | bytes 327680
  2167.3 312.2 %all-reduce.46.cloned.1.call-start = ((), (), s32[]{:S(2)}) async-start(), calls=%async_computation.28 | async-start | bytes 8388608 | tf_op jit(solution)/shard_map/psum | solution.py:285
  2177.9 337.9 %all-reduce.48.cloned.1.call-start = ((), (), s32[]{:S(2)}) async-start(), calls=%async_computation.29 | async-start | bytes 4259840 | tf_op jit(solution)/shard_map/psum | solution.py:400
  (134 other events, 1902.1 us)
Sparse Core Ops, SparseCore 0:
  9.9 30.1 all-gather.6
  41.9 27.5 all-gather.8
  71.3 26.4 all-gather.10
  712.5 155.2 all-reduce.41
  869.6 28.7 all-gather.12
  900.2 29.7 all-gather.14
  932.0 29.7 all-gather.16
  975.9 154.9 all-reduce.43
  1133.9 29.1 reduce-scatter.26
  1166.1 30.1 reduce-scatter.24
  1199.3 30.1 reduce-scatter.28
  2122.0 24.1 reduce-scatter.16
  2149.5 24.7 reduce-scatter.14
  2177.4 27.7 reduce-scatter.22
  2207.9 27.7 reduce-scatter.20
  2238.6 27.7 reduce-scatter.18
  2269.6 24.0 reduce-scatter.30
  2297.1 24.0 reduce-scatter.32
  2324.2 155.3 all-reduce.45
  2482.5 20.6 all-reduce.47
where the time goes:
time: 2560 us; the launch traced here: 2530 us
  other arithmetic  732 us (29%)
  matrix products  720 us (28%)
  waiting for transfers between devices  658 us (26%)
  local copies, waits for them, and re-layouts  308 us (12%)
  blocking collectives  79.4 us (3%)
    another operation x112, other arithmetic, group_step(): jax.scipy.linalg.solve_triangular(system, (beta_heads * from_start)[:, :,...  365 us
    another operation x64, other arithmetic, group_step(): jax.scipy.linalg.solve_triangular(system, beta_heads[:, :, None] * value_...  159 us
    psum x1, waiting for transfers between devices, body(): lax.psum(dot_plain(act_low, inner_down).astype(jnp.bfloat16), 'tp')  154 us
    psum x1, waiting for transfers between devices, body(): attn = lax.psum(dot_plain(mixed_low, output_full), 'tp')  153 us
    psum x1, waiting for transfers between devices, body(): grad_normed2 = lax.psum(part_second, 'tp')  139 us
    dynamic_update_slice x176, local copies, waits for them, and re-layouts, prepare(): lax.scan(group_step, start_state, (split(query), split(keys), split(widen...  130 us
    dot_general x48, matrix products, group_step(): jnp.einsum('hcd,hrd->hcr', query_heads, state, precision=HIGH)  88.1 us
    dot_general x48, matrix products, group_step(): jnp.einsum('hcr,hcd->hrd', update * to_end[:, :, None], key_heads, precis...  85.4 us
  transfers between devices with their start and end apart: 28, of which 14 were waited for; matrix products, arithmetic and copies ran while one was open for 68% of the time, Pallas kernels for 0%

commit v1 on v0

v1 whole, which is shorter than its diff:
```python
import jax
import jax.numpy as jnp
from jax import lax
from jax.sharding import PartitionSpec as P

GROUP = 128


HIGH = lax.Precision.HIGHEST
PRECISE = lax.Precision.HIGH


def from_behind(block, axis, distance):
    devices = range(lax.axis_size(axis))
    route = [(i - distance, i) for i in devices if i - distance in devices]
    return lax.ppermute(block, axis, route)


def dot_plain(left, right):
    return jnp.dot(left, right, preferred_element_type=jnp.float32)


def dot_first(left, right):
    return lax.dot_general(
        left, right, (((0,), (0,)), ((), ())), preferred_element_type=jnp.float32
    )


def dot_second(left, right):
    return lax.dot_general(
        left, right, (((1,), (1,)), ((), ())), preferred_element_type=jnp.float32
    )


def rms_norm(values, gain):
    return values * lax.rsqrt(jnp.mean(values * values, axis=-1, keepdims=True) + 1e-06) * gain


def unit_rows(values):
    return values * lax.rsqrt(jnp.sum(values * values, axis=-1, keepdims=True) + 1e-06)


def convolve(projected, rim_rows, weights, seg_ext):
    tok_rows = projected.shape[0]
    taps = weights.shape[0]
    extended = jnp.concatenate([rim_rows, projected], axis=0)
    seg_now = seg_ext[taps - 1 :]
    summed = jnp.zeros_like(projected)
    for offset in range(taps):
        begin = taps - 1 - offset
        linked = (seg_ext[begin : begin + tok_rows] == seg_now).astype(jnp.float32)
        summed = summed + weights[offset] * extended[begin : begin + tok_rows] * linked[:, None]
    return jax.nn.silu(summed)


def dot_high(equation, left, right):
    return jnp.einsum(equation, left, right, precision=PRECISE)


@jax.custom_vjp
def unit_lower_inverse(strict_part):
    size = strict_part.shape[-1]
    order = jnp.arange(size)
    above, across = order[:, None], order[None, :]
    inverse = jnp.broadcast_to(jnp.eye(size, dtype=jnp.float32), strict_part.shape)
    width = 1
    while width < size:
        paired = (above // (2 * width) == across // (2 * width)) & (
            above // width != across // width
        )
        coupling = jnp.where(paired, strict_part, 0.0)
        if width > 1:
            coupling = dot_high("...ij,...jk->...ik", coupling, inverse)
            coupling = dot_high("...ij,...jk->...ik", inverse, coupling)
        inverse = inverse - coupling
        width *= 2
    return inverse


def inverse_keep(strict_part):
    inverse = unit_lower_inverse(strict_part)
    return inverse, inverse


def inverse_pull(inverse, grad):
    inner = dot_high("...ij,...kj->...ik", grad, inverse)
    return (-dot_high("...ji,...jk->...ik", inverse, inner),)


unit_lower_inverse.defvjp(inverse_keep, inverse_pull)


def prepare(floats, seg_ext, key_dim, block_len):
    (
        q_proj,
        k_proj,
        v_proj,
        q_rim,
        k_rim,
        v_rim,
        a_proj,
        b_proj,
        q_conv,
        k_conv,
        v_conv,
        decay_log,
        decay_bias,
    ) = floats
    tok_rows = q_proj.shape[0]
    num_heads = a_proj.shape[1]
    taps = q_conv.shape[0]
    blocks = tok_rows // block_len

    def split(array):
        shaped = array.reshape(blocks, block_len, num_heads, -1)
        return jnp.transpose(shaped, (2, 0, 1, 3))

    query = unit_rows(split(convolve(q_proj, q_rim, q_conv, seg_ext))) * key_dim ** (-0.5)
    keys = unit_rows(split(convolve(k_proj, k_rim, k_conv, seg_ext)))
    values = split(convolve(v_proj, v_rim, v_conv, seg_ext))
    val_dim = values.shape[3]
    beta = jax.nn.sigmoid(b_proj).T.reshape(num_heads, blocks, block_len)
    log_gate = (-jnp.exp(decay_log) * jax.nn.softplus(a_proj + decay_bias)).T
    log_gate = log_gate.reshape(num_heads, blocks, block_len)
    seg_now = seg_ext[taps - 1 :].reshape(blocks, block_len)
    seg_before = seg_ext[taps - 2 : taps - 2 + tok_rows : block_len]
    order = jnp.arange(block_len)
    until = (order[:, None] <= order[None, :]).astype(jnp.float32)
    cumul = jnp.einsum("hcs,st->hct", log_gate, until, precision=HIGH)
    causal = (order[:, None] >= order[None, :]) & (seg_now[:, :, None] == seg_now[:, None, :])
    strict = causal & (order[:, None] > order[None, :])
    spacing = cumul[..., :, None] - cumul[..., None, :]
    within = jnp.where(causal, jnp.exp(jnp.where(causal, spacing, 0.0)), 0.0)
    from_start = jnp.where(seg_now == seg_before[:, None], jnp.exp(cumul), 0.0)
    to_end = within[..., -1, :]
    key_dots = dot_high("hctd,hcsd->hcts", keys, keys)
    inverse = unit_lower_inverse(jnp.where(strict, beta[..., None] * within * key_dots, 0.0))
    scores = dot_high("hctd,hcsd->hcts", query, keys) * within
    sources = jnp.concatenate(
        [(beta * from_start)[..., None] * keys, beta[..., None] * values], axis=-1
    )
    solved = dot_high("hcts,hcsx->hctx", inverse, sources)
    reached = dot_high("hcts,hcsx->hctx", scores, solved)
    moved = dot_high("hctx,hctd->hcxd", solved, keys * to_end[..., None])
    eye = jnp.eye(key_dim, dtype=jnp.float32)
    step_map = from_start[..., -1][..., None, None] * eye - moved[:, :, :key_dim]
    step_base = jnp.concatenate(
        [jnp.zeros((num_heads, blocks, key_dim, key_dim), jnp.float32), moved[:, :, key_dim:]],
        axis=2,
    )
    state = jnp.concatenate(
        [
            jnp.broadcast_to(eye, (num_heads, key_dim, key_dim)),
            jnp.zeros((num_heads, val_dim, key_dim), jnp.float32),
        ],
        axis=1,
    )
    states = []
    for block in range(blocks):
        states.append(state)
        state = dot_high("hxd,hde->hxe", state, step_map[:, block]) + step_base[:, block]
    entry = jnp.stack(states, axis=1)
    reading = from_start[..., None] * query - reached[..., :key_dim]
    outputs = dot_high("hctd,hcxd->hctx", reading, entry)
    mapped = outputs[..., :key_dim].reshape(num_heads, tok_rows, key_dim)
    base = (outputs[..., key_dim:] + reached[..., key_dim:]).reshape(num_heads, tok_rows, val_dim)
    return mapped, base, state[:, :key_dim], state[:, key_dim:]


def gated_out(core, gate_proj, gain):
    num_heads, tok_rows, val_dim = core.shape
    gating = jax.nn.silu(gate_proj.reshape(tok_rows, num_heads, val_dim))
    normed = rms_norm(core, gain)
    return (jnp.transpose(normed, (1, 0, 2)) * gating).reshape(tok_rows, -1)


def swish_product(gate_pre, up_pre):
    return jax.nn.silu(gate_pre) * up_pre


def add_tail(grad_rows, incoming):
    width = incoming.shape[0]
    return jnp.concatenate([grad_rows[:-width], grad_rows[-width:] + incoming], axis=0)


def body(
    tokens,
    segment_ids,
    cotangent,
    mixer_gain,
    query_weight,
    key_weight,
    value_weight,
    gate_weight,
    decay_weight,
    beta_weight,
    query_conv,
    key_conv,
    value_conv,
    decay_log,
    decay_bias,
    out_gain,
    output_weight,
    hidden_gain,
    hidden_gate,
    hidden_up,
    hidden_down,
):
    tok_rows = tokens.shape[0]
    num_heads = decay_log.shape[0]
    key_dim = query_weight.shape[1] // num_heads
    taps = query_conv.shape[0]
    range_count = lax.axis_size("ctx")
    begin_row = lax.axis_index("ctx") * tok_rows
    seg_pad = jnp.concatenate([jnp.full((taps - 1,), -1, jnp.int32), segment_ids[0]])
    seg_ext = lax.dynamic_slice_in_dim(seg_pad, begin_row, tok_rows + taps - 1)
    low = jnp.bfloat16
    heads_wide = num_heads * key_dim
    values_wide = value_weight.shape[1]
    mixer_wide = 2 * heads_wide + 2 * values_wide
    narrow_pad = jnp.zeros((query_weight.shape[0], -2 * num_heads % 128), low)
    mixer_full = lax.all_gather(
        jnp.concatenate(
            [
                query_weight,
                key_weight,
                value_weight,
                gate_weight,
                decay_weight,
                beta_weight,
                narrow_pad,
            ],
            axis=1,
        ),
        "shard",
        axis=0,
        tiled=True,
    )
    units = hidden_gate.shape[1]
    output_full = lax.all_gather(output_weight.T, "shard", axis=0, tiled=True)
    inner_full = lax.all_gather(
        jnp.concatenate([hidden_gate, hidden_up], axis=1), "shard", axis=0, tiled=True
    )
    down_full = lax.all_gather(hidden_down.T, "shard", axis=0, tiled=True)
    part_rows = tok_rows // lax.axis_size("tp")
    part_at = lax.axis_index("tp") * part_rows

    def own_rows(array):
        return lax.dynamic_slice_in_dim(array, part_at, part_rows)

    def sum_rows(array):
        summed = lax.psum_scatter(array.astype(low), "tp", scatter_dimension=0, tiled=True)
        return summed.astype(jnp.float32)

    def all_rows(array):
        return lax.all_gather(array, "tp", axis=0, tiled=True)

    normed_low = rms_norm(tokens.astype(jnp.float32), mixer_gain).astype(low)
    x_own = own_rows(tokens).astype(jnp.float32)
    _, norm_pull = jax.vjp(rms_norm, x_own, mixer_gain)
    projected = dot_plain(normed_low, mixer_full)
    q_proj = projected[:, :heads_wide]
    k_proj = projected[:, heads_wide : 2 * heads_wide]
    v_proj = projected[:, 2 * heads_wide : 2 * heads_wide + values_wide]
    z_proj = projected[:, 2 * heads_wide + values_wide : mixer_wide]
    a_proj = projected[:, mixer_wide : mixer_wide + num_heads]
    b_proj = projected[:, mixer_wide + num_heads : mixer_wide + 2 * num_heads]
    rim = from_behind(
        projected[tok_rows - taps + 1 :, : 2 * heads_wide + values_wide], "ctx", 1
    )
    q_rim = rim[:, :heads_wide]
    k_rim = rim[:, heads_wide : 2 * heads_wide]
    v_rim = rim[:, 2 * heads_wide :]

    def local_mixer(floats):
        return prepare(floats, seg_ext, key_dim, GROUP)

    (mapped_query, base_query, state_map, state_base), prep_pull = jax.vjp(
        local_mixer,
        (
            q_proj,
            k_proj,
            v_proj,
            q_rim,
            k_rim,
            v_rim,
            a_proj,
            b_proj,
            query_conv,
            key_conv,
            value_conv,
            decay_log,
            decay_bias,
        ),
    )
    state_in = jnp.zeros_like(state_base)
    for _ in range(range_count - 1):
        ends = dot_high("hvd,hde->hve", state_in, state_map) + state_base
        state_in = from_behind(ends, "ctx", 1)
    core = base_query + dot_high("hrd,hvd->hrv", mapped_query, state_in)
    mixed, post_pull = jax.vjp(gated_out, core, z_proj, out_gain)
    mixed_low = mixed.astype(low)
    middle = x_own + sum_rows(dot_second(mixed_low, output_full))
    normed2, norm2_pull = jax.vjp(rms_norm, middle, hidden_gain)
    normed2_low = all_rows(normed2.astype(low))
    inner = dot_plain(normed2_low, inner_full)
    act, act_pull = jax.vjp(swish_product, inner[:, :units], inner[:, units:])
    act_low = act.astype(low)
    grad_act = dot_plain(cotangent, down_full)
    grad_gate, grad_up = act_pull(grad_act)
    inner_low = jnp.concatenate([grad_gate.astype(low), grad_up.astype(low)], axis=1)
    grad_normed2 = sum_rows(dot_second(inner_low, inner_full))
    ffn = sum_rows(dot_second(act_low, down_full))
    block_out = all_rows((middle + ffn).astype(low))
    grad_down = dot_first(cotangent, act_low)
    grad_inner = dot_first(normed2_low, inner_low)
    grad_mid_norm, grad_hidden_gain = norm2_pull(grad_normed2)
    grad_middle = own_rows(cotangent).astype(jnp.float32) + grad_mid_norm
    attn_low = all_rows(grad_middle.astype(low))
    grad_output = dot_first(attn_low, mixed_low)
    grad_mixed = dot_plain(attn_low, output_full)
    grad_core, grad_z, grad_out_gain = post_pull(grad_mixed)
    direct = dot_high("hrv,hrd->hvd", grad_core, mapped_query)
    grad_end = jnp.zeros_like(direct)
    for _ in range(range_count - 1):
        totals = dot_high("hve,hde->hvd", grad_end, state_map) + direct
        grad_end = from_behind(totals.astype(low), "ctx", -1).astype(totals.dtype)
    grad_mapped = dot_high("hrv,hvd->hrd", grad_core, state_in)
    grad_map = dot_high("hvd,hve->hde", state_in, grad_end)
    (float_grads,) = prep_pull((grad_mapped, grad_core, grad_map, grad_end))
    (
        grad_q,
        grad_k,
        grad_v,
        grad_q_rim,
        grad_k_rim,
        grad_v_rim,
        grad_a,
        grad_b,
        grad_q_conv,
        grad_k_conv,
        grad_v_conv,
        grad_decay_log,
        grad_decay_bias,
    ) = float_grads
    back_rim = from_behind(
        jnp.concatenate([grad_q_rim, grad_k_rim, grad_v_rim], axis=1), "ctx", -1
    )
    conv_grad = add_tail(jnp.concatenate([grad_q, grad_k, grad_v], axis=1), back_rim)
    mixer_low = jnp.concatenate(
        [
            conv_grad.astype(low),
            grad_z.astype(low),
            grad_a.astype(low),
            grad_b.astype(low),
            jnp.zeros((tok_rows, narrow_pad.shape[1]), low),
        ],
        axis=1,
    )
    grad_normed = sum_rows(dot_second(mixer_low, mixer_full))
    grad_mixer = dot_first(normed_low, mixer_low)
    grad_x_norm, grad_mixer_gain = norm_pull(grad_normed)
    input_grad = all_rows((grad_middle + grad_x_norm).astype(low)).astype(jnp.float32)

    def sum_weight(array):
        part = lax.psum_scatter(array.astype(low), "shard", scatter_dimension=0, tiled=True)
        return lax.psum(part, "ctx").astype(jnp.float32)

    sum_inner = sum_weight(jnp.concatenate([grad_inner, grad_down, grad_output], axis=1))
    sum_mixer = sum_weight(grad_mixer)
    sum_mixer_gain, sum_hidden_gain, sum_out_gain = lax.psum(
        (grad_mixer_gain, grad_hidden_gain, grad_out_gain), ("shard", "ctx", "tp")
    )
    sum_q_conv, sum_k_conv, sum_v_conv, sum_decay_log, sum_decay_bias = lax.psum(
        (grad_q_conv, grad_k_conv, grad_v_conv, grad_decay_log, grad_decay_bias),
        ("shard", "ctx"),
    )
    return (
        block_out,
        input_grad,
        sum_mixer_gain,
        sum_mixer[:, :heads_wide],
        sum_mixer[:, heads_wide : 2 * heads_wide],
        sum_mixer[:, 2 * heads_wide : 2 * heads_wide + values_wide],
        sum_mixer[:, 2 * heads_wide + values_wide : mixer_wide],
        sum_mixer[:, mixer_wide : mixer_wide + num_heads],
        sum_mixer[:, mixer_wide + num_heads : mixer_wide + 2 * num_heads],
        sum_q_conv,
        sum_k_conv,
        sum_v_conv,
        sum_decay_log,
        sum_decay_bias,
        sum_out_gain,
        sum_inner[:, 3 * units :].T,
        sum_hidden_gain,
        sum_inner[:, :units],
        sum_inner[:, units : 2 * units],
        sum_inner[:, 2 * units : 3 * units].T,
    )


def solution(mesh):
    in_specs = (
        P(("shard", "ctx"), None),
        P("shard", None),
        P(("shard", "ctx"), None),
        P(),
        P("shard", "tp"),
        P("shard", "tp"),
        P("shard", "tp"),
        P("shard", "tp"),
        P("shard", "tp"),
        P("shard", "tp"),
        P(None, "tp"),
        P(None, "tp"),
        P(None, "tp"),
        P("tp"),
        P("tp"),
        P(),
        P("tp", "shard"),
        P(),
        P("shard", "tp"),
        P("shard", "tp"),
        P("tp", "shard"),
    )
    out_specs = (
        P(("shard", "ctx"), None),
        P(("shard", "ctx"), None),
        P(),
        P("shard", "tp"),
        P("shard", "tp"),
        P("shard", "tp"),
        P("shard", "tp"),
        P("shard", "tp"),
        P("shard", "tp"),
        P(None, "tp"),
        P(None, "tp"),
        P(None, "tp"),
        P("tp"),
        P("tp"),
        P(),
        P("tp", "shard"),
        P(),
        P("shard", "tp"),
        P("shard", "tp"),
        P("tp", "shard"),
    )
    return jax.shard_map(body, mesh=mesh, in_specs=in_specs, out_specs=out_specs, check_vma=False)
```

time: 2560 us -> 920 us (0.36)
  other arithmetic: 732 us -> 72.6 us
  matrix products: 720 us -> 161 us
  local copies, waits for them, and re-layouts: 308 us -> 101 us
  waiting for transfers between devices: 658 us -> 488 us
    another operation x251 -> x1, other arithmetic: 544 us -> 0.85 us  [the longest x112 365 us: group_step(): jax.scipy.linalg.solve_triangular(system, (beta_heads * from_start)[:, :,...]
    psum x4 -> x1, waiting for transfers between devices: 445 us -> 22.5 us  [sum_weight(): return lax.psum(part, 'ctx').astype(jnp.float32)]
    dot_general x326 -> x63, matrix products: 506 us -> 89.8 us  [the longest x59 86.7 us: dot_high(): return jnp.einsum(equation, left, right, precision=PRECISE)]
    reduce_scatter x8 -> x6, waiting for transfers between devices: 88.4 us -> 244 us  [the longest x4 133 us: sum_rows(): lax.psum_scatter(array.astype(low), 'tp', scatter_dimension=0, tiled=True)]
    all_gather x6 -> x8, waiting for transfers between devices: 76.1 us -> 219 us  [the longest x4 117 us: all_rows(): return lax.all_gather(array, 'tp', axis=0, tiled=True)]
    dynamic_update_slice x176 -> x0, local copies, waits for them, and re-layouts: 130 us -> none  [prepare(): lax.scan(group_step, start_state, (split(query), split(keys), split(widen...]
    another operation x96 -> x0, matrix products: 123 us -> none  [the longest x48 63.3 us: group_step(): jax.scipy.linalg.solve_triangular(system, beta_heads[:, :, None] * value_...]
    mul x69 -> x0, local copies, waits for them, and re-layouts: 58.6 us -> none  [the longest x16 20.1 us: group_step(): beta_heads[:, :, None] * value_heads]
  transfers between devices with their start and end apart: 28 -> 19, of which waited for: 14 -> 13; matrix products, arithmetic and copies ran while one was open for 68% -> 20% of each run, Pallas kernels for 0% -> 0%
where the time goes in v1:
time: 920 us; the launch traced here: 911 us
  waiting for transfers between devices  488 us (53%)
  matrix products  161 us (18%)
  local copies, waits for them, and re-layouts  101 us (11%)
  other arithmetic  72.6 us (8%)
  blocking collectives  65.5 us (7%)
  between operations  16.8 us (2%)
    reduce_scatter x4, waiting for transfers between devices, sum_rows(): lax.psum_scatter(array.astype(low), 'tp', scatter_dimension=0, tiled=True)  133 us
    all_gather x4, waiting for transfers between devices, all_rows(): return lax.all_gather(array, 'tp', axis=0, tiled=True)  117 us
    reduce_scatter x2, waiting for transfers between devices, sum_weight(): lax.psum_scatter(array.astype(low), 'shard', scatter_dimension=0, tiled=T...  111 us
    dot_general x59, matrix products, dot_high(): return jnp.einsum(equation, left, right, precision=PRECISE)  86.7 us
    all_gather x1, waiting for transfers between devices, body(): lax.all_gather(jnp.concatenate([query_weight, key_weight, value_weight, g...  42.8 us
    psum x1, blocking collectives, body(): lax.psum((grad_mixer_gain, grad_hidden_gain, grad_out_gain), ('shard', 'c...  41 us
    all_gather x1, waiting for transfers between devices, body(): lax.all_gather(jnp.concatenate([hidden_gate, hidden_up], axis=1), 'shard'...  37.6 us
    unnamed x387, local copies, waits for them, and re-layouts  35.2 us
  transfers between devices with their start and end apart: 19, of which 13 were waited for; matrix products, arithmetic and copies ran while one was open for 20% of the time, Pallas kernels for 0%

profile of v1, /device:TPU:0, one launch (start us, length us, event | category | flops | bytes accessed | tf_op | source)
XLA Modules:
  0.0 910.6 jit_solution(14726343507014059583)
XLA Ops:
  17.4 42.8 %all-gather.9.cloned.1.call-done = bf16[1024,1664]{1,0:T(8,128)(2,1)} async-done(((bf16[256,1664]{1,0:T(8,128)(2,1)}), bf16[1024,1664]{1,0:T(8,128)(2,1)}) %all-gather.9.cloned.1.call-update) | async-done | bytes 3407888 | tf_op jit(solution)/shard_map/all_gather | solution.py:222
  60.2 6.0 fusion.105
  156.7 41.9 %reduce-scatter.7.cloned.1.call-done = bf16[256,1024]{1,0:T(8,128)(2,1)} async-done(((bf16[1024,1024]{1,0:T(8,128)(2,1)}), bf16[256,1024]{1,0:T(8,128)(2,1)}) %reduce-scatter.7.cloned.1.call-update) | async-done | bytes 524304 | tf_op jit(solution)/shard_map/reduce_scatter | solution.py:252
  204.4 37.6 %all-gather.15.cloned.1.call-done = bf16[1024,1408]{0,1:T(8,128)(2,1)} async-done(((bf16[256,1408]{0,1:T(8,128)(2,1)}), bf16[1024,1408]{0,1:T(8,128)(2,1)}) %all-gather.15.cloned.1.call-update) | async-done | bytes 2883600 | tf_op jit(solution)/shard_map/all_gather | solution.py:241
  242.0 48.0 %all-gather.13.cloned.1.call-done = bf16[1024,1024]{1,0:T(8,128)(2,1)} async-done(((bf16[256,1024]{1,0:T(8,128)(2,1)}), bf16[1024,1024]{1,0:T(8,128)(2,1)}) %all-gather.13.cloned.1.call-update) | async-done | bytes 2097168 | tf_op jit(solution)/shard_map/all_gather | solution.py:256
  290.1 8.4 fusion.265
  298.5 21.9 %all-gather.17.cloned.1.call-done = bf16[1024,704]{0,1:T(8,128)(2,1)} async-done(((bf16[256,704]{0,1:T(8,128)(2,1)}), bf16[1024,704]{0,1:T(8,128)(2,1)}) %all-gather.17.cloned.1.call-update) | async-done | bytes 1441808 | tf_op jit(solution)/shard_map/all_gather | solution.py:244
  320.4 7.7 fusion.5
  334.7 44.0 %reduce-scatter.11.cloned.1.call-done = bf16[256,1024]{1,0:T(8,128)(2,1)} async-done(((bf16[1024,1024]{1,0:T(8,128)(2,1)}), bf16[256,1024]{1,0:T(8,128)(2,1)}) %reduce-scatter.11.cloned.1.call-update) | async-done | bytes 524304 | tf_op jit(solution)/shard_map/reduce_scatter | solution.py:252
  387.7 42.9 %all-gather.21.cloned.1.call-done = bf16[1024,1024]{1,0:T(8,128)(2,1)} async-done(((bf16[256,1024]{1,0:T(8,128)(2,1)}), bf16[1024,1024]{1,0:T(8,128)(2,1)}) %all-gather.21.cloned.1.call-update) | async-done | bytes 2097168 | tf_op jit(solution)/shard_map/all_gather | solution.py:256
  430.6 5.6 fusion.32
  451.5 6.0 fusion.264
  553.4 5.8 concatenate.60
  559.1 8.4 convolution_convert_fusion.2
  573.6 7.7 convolution_convert_fusion
  588.9 7.7 convolution_convert_fusion.1
  598.9 9.0 concatenate.61
  613.2 43.9 %reduce-scatter.9.cloned.1.call-done = bf16[256,1024]{1,0:T(8,128)(2,1)} async-done(((bf16[1024,1024]{1,0:T(8,128)(2,1)}), bf16[256,1024]{1,0:T(8,128)(2,1)}) %reduce-scatter.9.cloned.1.call-update) | async-done | bytes 524304 | tf_op jit(solution)/shard_map/reduce_scatter | solution.py:252
  660.9 44.8 %reduce-scatter.15.cloned.1.call-done = bf16[256,1664]{1,0:T(8,128)(2,1)} async-done(((bf16[1024,1664]{1,0:T(8,128)(2,1)}), bf16[256,1664]{1,0:T(8,128)(2,1)}) %reduce-scatter.15.cloned.1.call-update) | async-done | bytes 851984 | tf_op jit(solution)/shard_map/reduce_scatter | solution.py:366
  705.7 66.6 %reduce-scatter.17.cloned.1.call-done = bf16[256,2624]{1,0:T(8,128)(2,1)} async-done(((bf16[1024,2624]{1,0:T(8,128)(2,1)}), bf16[256,2624]{1,0:T(8,128)(2,1)}) %reduce-scatter.17.cloned.1.call-update) | async-done | bytes 1343504 | tf_op jit(solution)/shard_map/reduce_scatter | solution.py:366
  772.4 24.5 %all-reduce.53 = (f32[4,256]{1,0:T(4,128)}, f32[4,256]{1,0:T(4,128)}, f32[4,512]{1,0:T(4,128)}, f32[2]{0:T(128)}, f32[2]{0:T(128)}) all-reduce(f32[4,256]{1,0:T(4,128)S(1)} %pad_add_fusion.21, f32[4,256]{1,0:T(4,128)S(1)} %pad_add_fusion.20, ...), channel_id=1, replica_groups=mesh['shard'=4,'ctx'=2,'tp'=4] {'shard','ctx'}, use_global_device_ids=true, to_apply=%region_31.32 | all-reduce | flops 4100 | bytes 32800 | tf_op jit(solution)/shard_map/psum | solution.py:374
  796.8 41.0 %all-reduce.52 = (f32[1024]{0:T(1024)}, f32[256]{0:T(256)}, f32[1024]{0:T(1024)}) all-reduce(f32[1024]{0:T(1024)S(1)} %get-tuple-element.89, f32[256]{0:T(256)S(1)} %copy-done.167, f32[1024]{0:T(1024)S(1)} %copy-done.136), channel_id=1, replica_groups=mesh['shard'=4,'ctx'=2,'tp'=4] {'shard','ctx','tp'}, use_global_device_ids=true, to_apply=%region_24.25 | all-reduce | flops 2304 | bytes 18432 | tf_op jit(solution)/shard_map/psum | solution.py:371
  841.9 25.7 %all-gather.19.cloned.1.call-done = bf16[1024,1024]{1,0:T(8,128)(2,1)} async-done(((bf16[256,1024]{1,0:T(8,128)(2,1)}), bf16[1024,1024]{1,0:T(8,128)(2,1)}) %all-gather.19.cloned.1.call-update) | async-done | bytes 2097168 | tf_op jit(solution)/shard_map/all_gather | solution.py:256
  867.6 22.5 %all-reduce.57.cloned.1.call-done = (bf16[256,1664]{1,0:T(8,128)(2,1)}, bf16[256,2624]{1,0:T(8,128)(2,1)}) async-done(((bf16[256,1664]{1,0:T(8,128)(2,1)}, bf16[256,2624]{1,0:T(8,128)(2,1)}), (bf16[256,1664]{1,0:T(8,128)(2,1)}, bf16[256,2624]{1,0:T(8,128)(2,1)})) %all-reduce.57.cloned.1.call-update) | async-done | bytes 2195472 | tf_op jit(solution)/shard_map/psum | solution.py:367
  (620 shorter events, 273.4 us)
Async XLA Ops:
  7.2 53.0 %all-gather.9.cloned.1.call-start = ((), (), s32[]{:S(2)}) async-start(), calls=%async_computation.6 | async-start | bytes 4259840 | tf_op jit(solution)/shard_map/all_gather | solution.py:222
  11.2 139.1 %all-gather.11.cloned.1.call-start = ((), (), s32[]{:S(2)}) async-start(), calls=%async_computation.7 | async-start | bytes 1310720 | tf_op jit(solution)/shard_map/all_gather | solution.py:240
  11.9 186.7 %reduce-scatter.7.cloned.1.call-start = ((), (), s32[]{:S(2)}) async-start(), calls=%async_computation.8 | async-start | bytes 2621440 | tf_op jit(solution)/shard_map/reduce_scatter | solution.py:252
  12.1 103.2 %copy-start.75 = (f32[128,128]{1,0:T(8,128)}, f32[128,128]{1,0:T(8,128)S(1)}, u32[]{:S(2)}) copy-start(f32[128,128]{1,0:T(8,128)S(1)} %fusion.183) | copy-start | bytes 196612
  14.1 101.9 %copy-start.71 = (f32[2,128,128]{2,1,0:T(8,128)}, f32[2,128,128]{2,1,0:T(8,128)S(1)}, u32[]{:S(2)}) copy-start(f32[2,128,128]{2,1,0:T(8,128)S(1)} %broadcast_in_dim.210) | copy-start | bytes 393220
  71.2 7.0 collective-permute-start
  121.0 23.2 %collective-permute-start.1 = (f32[2,256,128]{2,1,0:T(8,128)}, f32[2,256,128]{2,1,0:T(8,128)S(1)}, u32[]{:S(2)}, u32[]{:S(2)}) collective-permute-start(f32[2,256,128]{2,1,0:T(8,128)} %convolution_add_fusion.20), channel_id=1, source_target_pairs={{0,4},{1,5},{2,6},{3,7},{8,12},{9,13},{10,14},{11,15},{16,20},{17,... | collective-permute-start | bytes 786440 | tf_op jit(solution)/shard_map/ppermute | solution.py:16
  154.6 87.4 %all-gather.15.cloned.1.call-start = ((), (), s32[]{:S(2)}) async-start(), calls=%async_computation.10 | async-start | bytes 3604480 | tf_op jit(solution)/shard_map/all_gather | solution.py:241
  156.7 133.4 %all-gather.13.cloned.1.call-start = ((), (), s32[]{:S(2)}) async-start(), calls=%async_computation.9 | async-start | bytes 2621440 | tf_op jit(solution)/shard_map/all_gather | solution.py:256
  203.4 117.0 %all-gather.17.cloned.1.call-start = ((), (), s32[]{:S(2)}) async-start(), calls=%async_computation.11 | async-start | bytes 1802240 | tf_op jit(solution)/shard_map/all_gather | solution.py:244
  204.0 174.7 %reduce-scatter.11.cloned.1.call-start = ((), (), s32[]{:S(2)}) async-start(), calls=%async_computation.14 | async-start | bytes 2621440 | tf_op jit(solution)/shard_map/reduce_scatter | solution.py:252
  334.6 96.0 %all-gather.21.cloned.1.call-start = ((), (), s32[]{:S(2)}) async-start(), calls=%async_computation.15 | async-start | bytes 2621440 | tf_op jit(solution)/shard_map/all_gather | solution.py:256
  385.2 226.5 %reduce-scatter.13.cloned.1.call-start = ((), (), s32[]{:S(2)}) async-start(), calls=%async_computation.16 | async-start | bytes 2621440 | tf_op jit(solution)/shard_map/reduce_scatter | solution.py:252
  450.2 32.4 %collective-permute-start.2 = (bf16[2,256,128]{2,1,0:T(8,128)(2,1)}, bf16[2,256,128]{2,1,0:T(8,128)(2,1)}, u32[]{:S(2)}, u32[]{:S(2)}) collective-permute-start(bf16[2,256,128]{2,1,0:T(8,128)(2,1)} %fusion.44), channel_id=1, source_target_pairs={{4,0},{5,1},{6,2},{7,3},{12,8},{13,9},{14,10},{15,11},{20,16},{21,... | collective-permute-start | bytes 393224 | tf_op jit(solution)/shard_map/ppermute | solution.py:16
  546.6 3.8 collective-permute-start.3
  567.5 89.6 %reduce-scatter.9.cloned.1.call-start = ((), (), s32[]{:S(2)}) async-start(), calls=%async_computation.12 | async-start | bytes 2621440 | tf_op jit(solution)/shard_map/reduce_scatter | solution.py:252
  572.0 133.7 %reduce-scatter.15.cloned.1.call-start = ((), (), s32[]{:S(2)}) async-start(), calls=%async_computation.18 | async-start | bytes 4259840 | tf_op jit(solution)/shard_map/reduce_scatter | solution.py:366
  581.3 191.0 %reduce-scatter.17.cloned.1.call-start = ((), (), s32[]{:S(2)}) async-start(), calls=%async_computation.19 | async-start | bytes 6881280 | tf_op jit(solution)/shard_map/reduce_scatter | solution.py:366
  608.0 229.8 %all-gather.23.cloned.1.call-start = ((), (), s32[]{:S(2)}) async-start(), calls=%async_computation.17 | async-start | bytes 2621440 | tf_op jit(solution)/shard_map/all_gather | solution.py:256
  660.3 112.1 %copy-start.181 = (f32[2]{0:T(128)S(1)}, f32[2]{0:T(128)}, u32[]{:S(2)}) copy-start(f32[2]{0:T(128)} %param.34) | copy-start | bytes 28
  660.3 136.6 %copy-start.136 = (f32[1024]{0:T(1024)S(1)}, f32[1024]{0:T(1024)}, u32[]{:S(2)}) copy-start(f32[1024]{0:T(1024)} %get-tuple-element.87) | copy-start | bytes 12292
  660.3 136.6 %copy-start.167 = (f32[256]{0:T(256)S(1)}, f32[256]{0:T(256)}, u32[]{:S(2)}) copy-start(f32[256]{0:T(256)} %get-tuple-element.82) | copy-start | bytes 3076
  660.3 207.3 %all-gather.19.cloned.1.call-start = ((), (), s32[]{:S(2)}) async-start(), calls=%async_computation.13 | async-start | bytes 2621440 | tf_op jit(solution)/shard_map/all_gather | solution.py:256
  660.9 229.2 %all-reduce.57.cloned.1.call-start = ((), (), s32[]{:S(2)}) async-start(), calls=%async_computation.20 | async-start | bytes 4456448 | tf_op jit(solution)/shard_map/psum | solution.py:367
  (182 other events, 1466.3 us)
Sparse Core Ops, SparseCore 0:
  11.3 48.8 all-gather.8
  62.0 26.4 all-gather.10
  154.7 43.8 reduce-scatter.6
  201.0 40.9 all-gather.14
  244.1 45.9 all-gather.12
  291.9 28.4 all-gather.16
  334.8 43.8 reduce-scatter.10
  385.3 45.2 all-gather.20
  567.7 43.9 reduce-scatter.12
  613.9 43.1 reduce-scatter.8
  660.2 45.4 reduce-scatter.14
  708.6 63.6 reduce-scatter.16
  774.4 46.3 all-gather.22
  822.8 44.7 all-gather.18
  869.9 20.1 all-reduce.56

commit v2 on v1

--- a/solution.py
+++ b/solution.py
@@ -218,8 +218,40 @@
     heads_wide = num_heads * key_dim
     values_wide = value_weight.shape[1]
     mixer_wide = 2 * heads_wide + 2 * values_wide
-    narrow_pad = jnp.zeros((query_weight.shape[0], -2 * num_heads % 128), low)
-    mixer_full = lax.all_gather(
+    narrow_pad = jnp.zeros((query_weight.shape[0], -(mixer_wide + 2 * num_heads) % 256), low)
+    paired = range_count == 2
+    partner = [(0, 1), (1, 0)]
+    core = lax.axis_index("ctx")
+
+    def swap(array):
+        return lax.ppermute(array, "ctx", partner)
+
+    def joined(own_half, other_half):
+        ahead = jnp.where(core == 0, own_half, other_half)
+        behind = jnp.where(core == 0, other_half, own_half)
+        return jnp.concatenate([ahead, behind], axis=1)
+
+    def half_of(array, index):
+        half = array.shape[1] // 2
+        return lax.dynamic_slice_in_dim(array, index * half, half, axis=1)
+
+    def gather_weight(array):
+        if not paired:
+            return lax.all_gather(array, "shard", axis=0, tiled=True)
+        own_half = lax.all_gather(half_of(array, core), "shard", axis=0, tiled=True)
+        return joined(own_half, swap(own_half))
+
+    def sum_weight(array):
+        array = array.astype(low)
+        if not paired:
+            part = lax.psum_scatter(array, "shard", scatter_dimension=0, tiled=True)
+            return lax.psum(part, "ctx").astype(jnp.float32)
+        incoming = swap(half_of(array, 1 - core))
+        own_half = half_of(array, core).astype(jnp.float32) + incoming.astype(jnp.float32)
+        part = lax.psum_scatter(own_half.astype(low), "shard", scatter_dimension=0, tiled=True)
+        return joined(part, swap(part)).astype(jnp.float32)
+
+    mixer_full = gather_weight(
         jnp.concatenate(
             [
                 query_weight,
@@ -231,17 +263,16 @@
                 narrow_pad,
             ],
             axis=1,
-        ),
-        "shard",
-        axis=0,
-        tiled=True,
+        )
     )
     units = hidden_gate.shape[1]
-    output_full = lax.all_gather(output_weight.T, "shard", axis=0, tiled=True)
-    inner_full = lax.all_gather(
-        jnp.concatenate([hidden_gate, hidden_up], axis=1), "shard", axis=0, tiled=True
-    )
-    down_full = lax.all_gather(hidden_down.T, "shard", axis=0, tiled=True)
+    later_wide = 3 * units + values_wide
+    later_pad = jnp.zeros((query_weight.shape[0], -later_wide % 256), low)
+    later_full = gather_weight(
+        jnp.concatenate(
+            [hidden_gate, hidden_up, hidden_down.T, output_weight.T, later_pad], axis=1
+        )
+    )
     part_rows = tok_rows // lax.axis_size("tp")
     part_at = lax.axis_index("tp") * part_rows
 
@@ -297,9 +328,12 @@
     for _ in range(range_count - 1):
         ends = dot_high("hvd,hde->hve", state_in, state_map) + state_base
         state_in = from_behind(ends, "ctx", 1)
-    core = base_query + dot_high("hrd,hvd->hrv", mapped_query, state_in)
-    mixed, post_pull = jax.vjp(gated_out, core, z_proj, out_gain)
-    mixed_low = mixed.astype(low)
+    heads_out = base_query + dot_high("hrd,hvd->hrv", mapped_query, state_in)
+    mixed, post_pull = jax.vjp(gated_out, heads_out, z_proj, out_gain)
+    mixed_low, later_full = lax.optimization_barrier((mixed.astype(low), later_full))
+    inner_full = later_full[:, : 2 * units]
+    down_full = later_full[:, 2 * units : 3 * units]
+    output_full = later_full[:, 3 * units : later_wide]
     middle = x_own + sum_rows(dot_second(mixed_low, output_full))
     normed2, norm2_pull = jax.vjp(rms_norm, middle, hidden_gain)
     normed2_low = all_rows(normed2.astype(low))
@@ -310,14 +344,19 @@
     grad_gate, grad_up = act_pull(grad_act)
     inner_low = jnp.concatenate([grad_gate.astype(low), grad_up.astype(low)], axis=1)
     grad_normed2 = sum_rows(dot_second(inner_low, inner_full))
-    ffn = sum_rows(dot_second(act_low, down_full))
+    grad_mid_norm, grad_hidden_gain = norm2_pull(grad_normed2)
+    grad_middle = own_rows(cotangent).astype(jnp.float32) + grad_mid_norm
+    attn_low = all_rows(grad_middle.astype(low))
+    act_late, attn_low = lax.optimization_barrier((act_low, attn_low))
+    ffn = sum_rows(dot_second(act_late, down_full))
     block_out = all_rows((middle + ffn).astype(low))
     grad_down = dot_first(cotangent, act_low)
     grad_inner = dot_first(normed2_low, inner_low)
-    grad_mid_norm, grad_hidden_gain = norm2_pull(grad_normed2)
-    grad_middle = own_rows(cotangent).astype(jnp.float32) + grad_mid_norm
-    attn_low = all_rows(grad_middle.astype(low))
     grad_output = dot_first(attn_low, mixed_low)
+    later_zeros = jnp.zeros((tokens.shape[1], later_pad.shape[1]), jnp.float32)
+    sum_later = sum_weight(
+        jnp.concatenate([grad_inner, grad_down, grad_output, later_zeros], axis=1)
+    )
     grad_mixed = dot_plain(attn_low, output_full)
     grad_core, grad_z, grad_out_gain = post_pull(grad_mixed)
     direct = dot_high("hrv,hrd->hvd", grad_core, mapped_query)
@@ -357,16 +396,12 @@
         ],
         axis=1,
     )
+    mixer_low, block_out, sum_later = lax.optimization_barrier((mixer_low, block_out, sum_later))
     grad_normed = sum_rows(dot_second(mixer_low, mixer_full))
     grad_mixer = dot_first(normed_low, mixer_low)
     grad_x_norm, grad_mixer_gain = norm_pull(grad_normed)
     input_grad = all_rows((grad_middle + grad_x_norm).astype(low)).astype(jnp.float32)
 
-    def sum_weight(array):
-        part = lax.psum_scatter(array.astype(low), "shard", scatter_dimension=0, tiled=True)
-        return lax.psum(part, "ctx").astype(jnp.float32)
-
-    sum_inner = sum_weight(jnp.concatenate([grad_inner, grad_down, grad_output], axis=1))
     sum_mixer = sum_weight(grad_mixer)
     sum_mixer_gain, sum_hidden_gain, sum_out_gain = lax.psum(
         (grad_mixer_gain, grad_hidden_gain, grad_out_gain), ("shard", "ctx", "tp")
@@ -391,11 +426,11 @@
         sum_decay_log,
         sum_decay_bias,
         sum_out_gain,
-        sum_inner[:, 3 * units :].T,
+        sum_later[:, 3 * units : later_wide].T,
         sum_hidden_gain,
-        sum_inner[:, :units],
-        sum_inner[:, units : 2 * units],
-        sum_inner[:, 2 * units : 3 * units].T,
+        sum_later[:, :units],
+        sum_later[:, units : 2 * units],
+        sum_later[:, 2 * units : 3 * units].T,
     )
 
 

time: 920 us -> 761 us (0.83)
  waiting for transfers between devices: 488 us -> 288 us
  other arithmetic: 72.6 us -> 94 us
  local copies, waits for them, and re-layouts: 101 us -> 115 us
    reduce_scatter x2, waiting for transfers between devices: 111 us -> 6.72 us  [sum_weight(): lax.psum_scatter(own_half.astype(low), 'shard', scatter_dimension=0, tile...]
    all_gather x4 -> x2, waiting for transfers between devices: 102 us -> 73.5 us  [gather_weight(): own_half = lax.all_gather(half_of(array, core), 'shard', axis=0, tiled=True)]
    all_gather x4, waiting for transfers between devices: 117 us -> 88.6 us  [all_rows(): return lax.all_gather(array, 'tp', axis=0, tiled=True)]
    psum x1 -> x0, waiting for transfers between devices: 22.5 us -> none  [sum_weight(): return lax.psum(part, 'ctx').astype(jnp.float32)]
    reduce_scatter x4, waiting for transfers between devices: 133 us -> 115 us  [sum_rows(): lax.psum_scatter(array.astype(low), 'tp', scatter_dimension=0, tiled=True)]
    unnamed x387 -> x433, local copies, waits for them, and re-layouts: 35.2 us -> 37.4 us
  transfers between devices with their start and end apart: 19 -> 22, of which waited for: 13 -> 10; matrix products, arithmetic and copies ran while one was open for 20% -> 34% of each run, Pallas kernels for 0% -> 0%
where the time goes in v2:
time: 761 us; the launch traced here: 751 us
  waiting for transfers between devices  288 us (38%)
  matrix products  158 us (21%)
  local copies, waits for them, and re-layouts  115 us (15%)
  other arithmetic  94 us (12%)
  blocking collectives  67.4 us (9%)
  between operations  17.6 us (2%)
  starting transfers between devices  10.9 us (1%)
    reduce_scatter x4, waiting for transfers between devices, sum_rows(): lax.psum_scatter(array.astype(low), 'tp', scatter_dimension=0, tiled=True)  115 us
    dot_general x59, matrix products, dot_high(): return jnp.einsum(equation, left, right, precision=PRECISE)  89 us
    all_gather x4, waiting for transfers between devices, all_rows(): return lax.all_gather(array, 'tp', axis=0, tiled=True)  88.6 us
    all_gather x2, waiting for transfers between devices, gather_weight(): own_half = lax.all_gather(half_of(array, core), 'shard', axis=0, tiled=True)  73.5 us
    psum x1, blocking collectives, body(): lax.psum((grad_mixer_gain, grad_hidden_gain, grad_out_gain), ('shard', 'c...  42.3 us
    unnamed x433, local copies, waits for them, and re-layouts  37.4 us
    psum x1, blocking collectives, body(): lax.psum((grad_q_conv, grad_k_conv, grad_v_conv, grad_decay_log, grad_dec...  25.1 us
    dot_general x4, matrix products, dot_first(): lax.dot_general(left, right, (((0,), (0,)), ((), ())), preferred_element_...  23.2 us
  transfers between devices with their start and end apart: 22, of which 10 were waited for; matrix products, arithmetic and copies ran while one was open for 34% of the time, Pallas kernels for 0%

profile of v2, /device:TPU:0, one launch (start us, length us, event | category | flops | bytes accessed | tf_op | source)
XLA Modules:
  0.0 750.8 jit_solution(13053609407177853542)
XLA Ops:
  13.6 33.6 %all-gather.7.cloned.1.call-done = bf16[1024,896]{1,0:T(8,128)(2,1)} async-done(((bf16[256,896]{1,0:T(8,128)(2,1)}), bf16[1024,896]{1,0:T(8,128)(2,1)}) %all-gather.7.cloned.1.call-update) | async-done | bytes 1835024 | tf_op jit(solution)/shard_map/all_gather | solution.py:241
  51.4 39.9 %all-gather.9.cloned.1.call-done = bf16[1024,1408]{0,1:T(8,128)(2,1)} async-done(((bf16[256,1408]{0,1:T(8,128)(2,1)}), bf16[1024,1408]{0,1:T(8,128)(2,1)}) %all-gather.9.cloned.1.call-update) | async-done | bytes 2883600 | tf_op jit(solution)/shard_map/all_gather | solution.py:241
  117.3 4.3 fusion.99
  188.9 44.0 %reduce-scatter.7.cloned.1.call-done = bf16[256,1024]{1,0:T(8,128)(2,1)} async-done(((bf16[1024,1024]{1,0:T(8,128)(2,1)}), bf16[256,1024]{1,0:T(8,128)(2,1)}) %reduce-scatter.7.cloned.1.call-update) | async-done | bytes 524304 | tf_op jit(solution)/shard_map/reduce_scatter | solution.py:283
  237.9 45.1 %all-gather.11.cloned.1.call-done = bf16[1024,1024]{1,0:T(8,128)(2,1)} async-done(((bf16[256,1024]{1,0:T(8,128)(2,1)}), bf16[1024,1024]{1,0:T(8,128)(2,1)}) %all-gather.11.cloned.1.call-update) | async-done | bytes 2097168 | tf_op jit(solution)/shard_map/all_gather | solution.py:287
  283.0 6.0 fusion.22
  289.1 5.4 fusion.5
  296.2 4.7 fusion.46
  301.0 42.7 %reduce-scatter.9.cloned.1.call-done = bf16[256,1024]{1,0:T(8,128)(2,1)} async-done(((bf16[1024,1024]{1,0:T(8,128)(2,1)}), bf16[256,1024]{1,0:T(8,128)(2,1)}) %reduce-scatter.9.cloned.1.call-update) | async-done | bytes 524304 | tf_op jit(solution)/shard_map/reduce_scatter | solution.py:283
  352.5 4.9 fusion.50
  360.4 7.6 %convolution_convert_fusion = bf16[1024,1408]{1,0:T(8,128)(2,1)} fusion(bf16[1024,1024]{1,0:T(8,128)(2,1)} %all-gather.11.cloned.1.call-done, bf16[1024,704]{1,0:T(8,128)(2,1)} %copy-done.200, bf16[1024,704]{1,0:T(8,128)(2,1)} %copy-done.199), kind=kOutput, calls=%fused_computation.18 | convolution fusion | flops 2959998976 | bytes 7864320 | tf_op jit(solution)/shard_map/dot_general | solution.py:24
  367.9 27.6 %all-gather.13.cloned.1.call-done = bf16[1024,1024]{1,0:T(8,128)(2,1)} async-done(((bf16[256,1024]{1,0:T(8,128)(2,1)}), bf16[1024,1024]{1,0:T(8,128)(2,1)}) %all-gather.13.cloned.1.call-update) | async-done | bytes 2097168 | tf_op jit(solution)/shard_map/all_gather | solution.py:287
  416.2 6.4 fusion.279
  425.7 4.5 convolution_convert_fusion.3
  435.7 5.3 fusion.19
  454.7 9.9 %concatenate.75 = bf16[1024,2816]{1,0:T(8,128)(2,1)} concatenate(bf16[1024,1408]{1,0:T(8,128)(2,1)} %convolution_convert_fusion, bf16[1024,704]{1,0:T(8,128)(2,1)} %copy.272, bf16[1024,512]{1,0:T(8,128)(2,1)} %convolution_convert_fusion.5, bf16[1024,192]{1,0:T(8,128)(2,1)} %broadcast_in_dim.241), dimensions={1} | concatenate | bytes 11534336 | tf_op jit(solution)/shard_map/concatenate | solution.py:358
  572.3 6.1 concatenate.74
  581.6 15.9 %all-gather.15.cloned.1.call-done = bf16[1024,1024]{1,0:T(8,128)(2,1)} async-done(((bf16[256,1024]{1,0:T(8,128)(2,1)}), bf16[1024,1024]{1,0:T(8,128)(2,1)}) %all-gather.15.cloned.1.call-update) | async-done | bytes 2097168 | tf_op jit(solution)/shard_map/all_gather | solution.py:287
  597.5 7.9 %fusion.45 = bf16[1024,1024]{1,0:T(8,128)(2,1)} fusion(bf16[1024,1792]{1,0:T(8,128)(2,1)} %concatenate.74, bf16[1024,896]{1,0:T(8,128)(2,1)} %copy-done.92, bf16[1024,896]{1,0:T(8,128)(2,1)S(1)} %copy-done.91), kind=kOutput, calls=%fused_computation.111 | convolution fusion | flops 3766484992 | bytes 9437184 | tf_op jit(solution)/shard_map/dot_general | solution.py:30
  607.0 6.5 convolution_convert_fusion.1
  619.5 28.7 %reduce-scatter.15.cloned.1.call-done = bf16[256,1024]{1,0:T(8,128)(2,1)} async-done(((bf16[1024,1024]{1,0:T(8,128)(2,1)}), bf16[256,1024]{1,0:T(8,128)(2,1)}) %reduce-scatter.15.cloned.1.call-update) | async-done | bytes 524304 | tf_op jit(solution)/shard_map/reduce_scatter | solution.py:283
  652.6 25.1 %all-reduce.53 = (f32[4,256]{1,0:T(4,128)}, f32[4,256]{1,0:T(4,128)}, f32[4,512]{1,0:T(4,128)}, f32[2]{0:T(128)}, f32[2]{0:T(128)}) all-reduce(f32[4,256]{1,0:T(4,128)S(1)} %pad_add_fusion.21, f32[4,256]{1,0:T(4,128)S(1)} %pad_add_fusion.20, ...), channel_id=1, replica_groups=mesh['shard'=4,'ctx'=2,'tp'=4] {'shard','ctx'}, use_global_device_ids=true, to_apply=%region_31.32 | all-reduce | flops 4100 | bytes 32800 | tf_op jit(solution)/shard_map/psum | solution.py:409
  677.7 6.7 reduce-scatter.17.cloned.1.call-done
  692.1 42.3 %all-reduce.52 = (f32[1024]{0:T(1024)}, f32[256]{0:T(256)}, f32[1024]{0:T(1024)}) all-reduce(f32[1024]{0:T(1024)S(1)} %get-tuple-element.103, f32[256]{0:T(256)S(1)} %copy-done.186, f32[1024]{0:T(1024)S(1)} %copy-done.157), channel_id=1, replica_groups=mesh['shard'=4,'ctx'=2,'tp'=4] {'shard','ctx','tp'}, use_global_device_ids=true, to_apply=%region_25.26 | all-reduce | flops 2304 | bytes 18432 | tf_op jit(solution)/shard_map/psum | solution.py:406
  (684 shorter events, 302.2 us)
Async XLA Ops:
  7.2 40.0 %all-gather.7.cloned.1.call-start = ((), (), s32[]{:S(2)}) async-start(), calls=%async_computation.6 | async-start | bytes 2293760 | tf_op jit(solution)/shard_map/all_gather | solution.py:241
  11.2 80.1 %all-gather.9.cloned.1.call-start = ((), (), s32[]{:S(2)}) async-start(), calls=%async_computation.7 | async-start | bytes 3604480 | tf_op jit(solution)/shard_map/all_gather | solution.py:241
  12.4 220.4 %reduce-scatter.7.cloned.1.call-start = ((), (), s32[]{:S(2)}) async-start(), calls=%async_computation.8 | async-start | bytes 2621440 | tf_op jit(solution)/shard_map/reduce_scatter | solution.py:283
  12.8 143.2 %copy-start.94 = (f32[128,128]{1,0:T(8,128)}, f32[128,128]{1,0:T(8,128)S(1)}, u32[]{:S(2)}) copy-start(f32[128,128]{1,0:T(8,128)S(1)} %fusion.199) | copy-start | bytes 196612
  12.8 143.9 %copy-start.86 = (f32[2,128,128]{2,1,0:T(8,128)}, f32[2,128,128]{2,1,0:T(8,128)S(1)}, u32[]{:S(2)}) copy-start(f32[2,128,128]{2,1,0:T(8,128)S(1)} %broadcast_in_dim.216) | copy-start | bytes 393220
  47.2 44.1 %collective-permute-start = (bf16[1024,896]{1,0:T(8,128)(2,1)}, bf16[1024,896]{1,0:T(8,128)(2,1)}, u32[]{:S(2)}, u32[]{:S(2)}) collective-permute-start(bf16[1024,896]{1,0:T(8,128)(2,1)} %all-gather.7.cloned.1.call-done), channel_id=1, source_target_pairs={{0,4},{4,0},{1,5},{5,1},{2,6},{6,2},{3,7},{7,3},{8,12},{12,8},{9,1... | collective-permute-start | bytes 5505032 | tf_op jit(solution)/shard_map/ppermute | solution.py:227
  91.3 87.9 %collective-permute-start.3 = (bf16[1024,1408]{0,1:T(8,128)(2,1)}, bf16[1024,1408]{0,1:T(8,128)(2,1)}, u32[]{:S(2)}, u32[]{:S(2)}) collective-permute-start(bf16[1024,1408]{0,1:T(8,128)(2,1)} %all-gather.9.cloned.1.call-done), channel_id=1, source_target_pairs={{0,4},{4,0},{1,5},{5,1},{2,6},{6,2},{3,7},{7,3},{8,12},{12,8},{9,1... | collective-permute-start | bytes 8650760 | tf_op jit(solution)/shard_map/ppermute | solution.py:227
  102.3 8.2 %collective-permute-start.1 = (f32[3,1024]{1,0:T(4,128)S(1)}, f32[3,1024]{1,0:T(4,128)}, u32[]{:S(2)}, u32[]{:S(2)}) collective-permute-start(f32[3,1024]{1,0:T(4,128)S(1)} %slice.331), channel_id=1, source_target_pairs={{0,4},{1,5},{2,6},{3,7},{8,12},{9,13},{10,14},{11,15},{16,20},{17,... | collective-permute-start | bytes 36872 | tf_op jit(solution)/shard_map/ppermute | solution.py:16
  161.6 13.2 %collective-permute-start.2 = (f32[2,256,128]{2,1,0:T(8,128)}, f32[2,256,128]{2,1,0:T(8,128)S(1)}, u32[]{:S(2)}, u32[]{:S(2)}) collective-permute-start(f32[2,256,128]{2,1,0:T(8,128)} %convolution_add_fusion.20), channel_id=1, source_target_pairs={{0,4},{1,5},{2,6},{3,7},{8,12},{9,13},{10,14},{11,15},{16,20},{17,... | collective-permute-start | bytes 786440 | tf_op jit(solution)/shard_map/ppermute | solution.py:16
  188.8 94.2 %all-gather.11.cloned.1.call-start = ((), (), s32[]{:S(2)}) async-start(), calls=%async_computation.9 | async-start | bytes 2621440 | tf_op jit(solution)/shard_map/all_gather | solution.py:287
  237.6 106.0 %reduce-scatter.9.cloned.1.call-start = ((), (), s32[]{:S(2)}) async-start(), calls=%async_computation.10 | async-start | bytes 2621440 | tf_op jit(solution)/shard_map/reduce_scatter | solution.py:283
  300.9 94.7 %all-gather.13.cloned.1.call-start = ((), (), s32[]{:S(2)}) async-start(), calls=%async_computation.11 | async-start | bytes 2621440 | tf_op jit(solution)/shard_map/all_gather | solution.py:287
  350.2 193.3 %reduce-scatter.11.cloned.1.call-start = ((), (), s32[]{:S(2)}) async-start(), calls=%async_computation.12 | async-start | bytes 2621440 | tf_op jit(solution)/shard_map/reduce_scatter | solution.py:283
  432.4 131.9 %reduce-scatter.13.cloned.1.call-start = ((), (), s32[]{:S(2)}) async-start(), calls=%async_computation.14 | async-start | bytes 3604480 | tf_op jit(solution)/shard_map/reduce_scatter | solution.py:251
  434.4 40.7 %collective-permute-start.4 = (bf16[2,256,128]{2,1,0:T(8,128)(2,1)}, bf16[2,256,128]{2,1,0:T(8,128)(2,1)}, u32[]{:S(2)}, u32[]{:S(2)}) collective-permute-start(bf16[2,256,128]{2,1,0:T(8,128)(2,1)} %fusion.58), channel_id=1, source_target_pairs={{4,0},{5,1},{6,2},{7,3},{12,8},{13,9},{14,10},{15,11},{20,16},{21,... | collective-permute-start | bytes 393224 | tf_op jit(solution)/shard_map/ppermute | solution.py:16
  473.7 32.2 %collective-permute-start.6 = (bf16[1024,1408]{1,0:T(8,128)(2,1)}, bf16[1024,1408]{1,0:T(8,128)(2,1)S(1)}, u32[]{:S(2)}, u32[]{:S(2)}) collective-permute-start(bf16[1024,1408]{1,0:T(8,128)(2,1)} %constant_dynamic-slice_fusion.1), channel_id=1, source_target_pairs={{0,4},{4,0},{1,5},{5,1},{2,6},{6,2},{3,7},{7,3},{8,12},{12,8},{9,1... | collective-permute-start | bytes 8650760 | tf_op jit(solution)/shard_map/ppermute | solution.py:227
  508.5 89.1 %all-gather.15.cloned.1.call-start = ((), (), s32[]{:S(2)}) async-start(), calls=%async_computation.13 | async-start | bytes 2621440 | tf_op jit(solution)/shard_map/all_gather | solution.py:287
  545.8 102.4 %reduce-scatter.15.cloned.1.call-start = ((), (), s32[]{:S(2)}) async-start(), calls=%async_computation.15 | async-start | bytes 2621440 | tf_op jit(solution)/shard_map/reduce_scatter | solution.py:283
  561.2 9.2 %collective-permute-start.5 = (f32[3,1024]{1,0:T(4,128)S(1)}, f32[3,1024]{1,0:T(4,128)S(1)}, u32[]{:S(2)}, u32[]{:S(2)}) collective-permute-start(f32[3,1024]{1,0:T(4,128)S(1)} %pad_maximum_fusion.17), channel_id=1, source_target_pairs={{4,0},{5,1},{6,2},{7,3},{12,8},{13,9},{14,10},{15,11},{20,16},{21,... | collective-permute-start | bytes 36872 | tf_op jit(solution)/shard_map/ppermute | solution.py:16
  564.3 14.0 %collective-permute-start.7 = (bf16[256,1408]{1,0:T(8,128)(2,1)}, bf16[256,1408]{1,0:T(8,128)(2,1)}, u32[]{:S(2)}, u32[]{:S(2)}) collective-permute-start(bf16[256,1408]{1,0:T(8,128)(2,1)} %reduce-scatter.13.cloned.1.call-done), channel_id=1, source_target_pairs={{0,4},{4,0},{1,5},{5,1},{2,6},{6,2},{3,7},{7,3},{8,12},{12,8},{9,1... | collective-permute-start | bytes 2162696 | tf_op jit(solution)/shard_map/ppermute | solution.py:227
  605.5 79.0 %reduce-scatter.17.cloned.1.call-start = ((), (), s32[]{:S(2)}) async-start(), calls=%async_computation.17 | async-start | bytes 2293760 | tf_op jit(solution)/shard_map/reduce_scatter | solution.py:251
  613.7 3.9 collective-permute-start.8
  619.4 118.5 %all-gather.17.cloned.1.call-start = ((), (), s32[]{:S(2)}) async-start(), calls=%async_computation.16 | async-start | bytes 2621440 | tf_op jit(solution)/shard_map/all_gather | solution.py:287
  684.4 49.9 %collective-permute-start.9 = (bf16[256,896]{1,0:T(8,128)(2,1)}, bf16[256,896]{1,0:T(8,128)(2,1)S(1)}, u32[]{:S(2)}, u32[]{:S(2)}) collective-permute-start(bf16[256,896]{1,0:T(8,128)(2,1)} %reduce-scatter.17.cloned.1.call-done), channel_id=1, source_target_pairs={{0,4},{4,0},{1,5},{5,1},{2,6},{6,2},{3,7},{7,3},{8,12},{12,8},{9,1... | collective-permute-start | bytes 1376264 | tf_op jit(solution)/shard_map/ppermute | solution.py:227
  (206 other events, 1860.7 us)
Sparse Core Ops, SparseCore 0:
  11.3 35.8 all-gather.6
  49.6 41.6 all-gather.8
  189.0 43.8 reduce-scatter.6
  237.8 45.2 all-gather.10
  301.0 42.5 reduce-scatter.8
  350.3 45.2 all-gather.12
  432.6 42.5 reduce-scatter.10
  508.6 40.7 reduce-scatter.12
  551.5 45.9 all-gather.14
  605.6 42.5 reduce-scatter.14
  651.8 32.5 reduce-scatter.16
  686.4 46.9 all-gather.16
